TPU v7x, 768 devices: a whole 4x8x12 slice. The times are simulated.
768 devices in a mesh: ctx: 24 (over x_hi, z), exp: 32 (over y, x_lo, core).
Axes of the slice: x: 4 (x_hi: 2, x_lo: 2; x = x_hi * 2 + x_lo), y: 8, z: 12, core: 2. Of those that a mesh axis runs over, the one named last changes fastest.
Arguments:
- queries: bfloat16 [32, 1536, 1024], P('exp', 'ctx'), may hold values from -6 to 6
- keys: bfloat16 [32, 1536, 1024], P('exp', 'ctx'), may hold values from -6 to 6
- values: bfloat16 [32, 1536, 1024], P('exp', 'ctx'), may hold values from -6 to 6
- residual: bfloat16 [32, 1536, 2048], P('exp', 'ctx'), may hold values from -6 to 6
- out_proj: bfloat16 [1024, 2048], replicated, may hold values from -0.1875 to 0.1875
- norm_gain: float32 [2048], replicated, may hold values from 0.25 to 1.75
- w_gate: bfloat16 [32, 2048, 512], P('exp'), may hold values from -0.125 to 0.125
- w_up: bfloat16 [32, 2048, 512], P('exp'), may hold values from -0.125 to 0.125
- w_down: bfloat16 [32, 512, 2048], P('exp'), may hold values from -0.25 to 0.25
- routes: int32 [32, 1536, 4], P('exp', 'ctx'), may hold values from 0 to 31, all different within a row; in each aligned block of 64 rows (0 to 63, 64 to 127, ..., all dimensions but the last counted through in order) at most 12 rows name the same one
- route_prob: float32 [32, 1536, 4], P('exp', 'ctx'), may hold values from 0.05 to 0.8
Outputs:
- mixed: bfloat16 [32, 1536, 2048], P('exp', 'ctx')
Inputs may be any that keep to these rules, and one draw needn't show every extreme that they name: `routes`: each row names 4 different experts; the 64 rows of one device name no expert more than 12 times, and in some devices' rows one expert exactly 12 times.
All inputs are finite; a program needn't handle non-finite values.
Results may differ from a plain program's by a relative error of at most 0.008.
Values may be sent and summed in bfloat16 or wider, within the bound.
No kernel may reach another device: no remote copies, remote signals or barrier semaphores. Data moves between devices by JAX's collectives and lax.ppermute only.
A program may use at most 64 MiB of HBM per device.

v0:
```python
import jax
import jax.numpy as jnp
from jax import lax
from jax.sharding import PartitionSpec as P

HEADS = 8
HEAD_DIM = 128
TOP = 4


neg_big = -1e30


def attend_piece(softmax_state, query_heads, query_pos, key_piece):
    run_max, run_sum, run_acc = softmax_state
    length = key_piece.shape[1]
    key_rows = key_piece[0].reshape(length, HEADS, HEAD_DIM)
    value_rows = key_piece[1].reshape(length, HEADS, HEAD_DIM)
    scale = HEAD_DIM ** (-0.5)
    scores = jnp.einsum("hqd,khd->hqk", query_heads, key_rows, preferred_element_type=jnp.float32)
    key_pos = jnp.arange(length, dtype=jnp.int32)
    allowed = key_pos[None, :] <= query_pos[:, None]
    scores = jnp.where(allowed[None], scores, neg_big)
    new_max = jnp.maximum(run_max, scores.max(axis=-1))
    rescale = jnp.exp((run_max - new_max) * scale)
    exponent = jnp.where(allowed[None], jnp.exp((scores - new_max[:, :, None]) * scale), 0.0)
    run_sum = run_sum * rescale + exponent.sum(axis=-1)
    update = jnp.einsum(
        "hqk,khd->hqd",
        exponent.astype(jnp.bfloat16),
        value_rows,
        preferred_element_type=jnp.float32,
    )
    run_acc = run_acc * rescale[:, :, None] + update
    return (new_max, run_sum, run_acc)


def local(
    queries, keys, values, residual, out_proj, norm_gain, w_gate, w_up, w_down, routes, route_prob
):
    tok_count = queries.shape[1]
    my_index = lax.axis_index("ctx")
    query_pos = my_index * tok_count + jnp.arange(tok_count, dtype=jnp.int32)
    query_heads = jnp.transpose(queries[0].reshape(tok_count, HEADS, HEAD_DIM), (1, 0, 2))
    stacked = jnp.stack([keys[0], values[0]])
    start_state = (
        jnp.full((HEADS, tok_count), neg_big, jnp.float32),
        jnp.zeros((HEADS, tok_count), jnp.float32),
        jnp.zeros((HEADS, tok_count, HEAD_DIM), jnp.float32),
    )
    key_piece = lax.all_gather(stacked, "ctx", axis=1, tiled=True)
    final_state = attend_piece(start_state, query_heads, query_pos, key_piece)
    run_max, run_sum, run_acc = final_state
    attended_heads = (run_acc / run_sum[:, :, None]).astype(jnp.bfloat16)
    attended = jnp.transpose(attended_heads, (1, 0, 2)).reshape(tok_count, HEADS * HEAD_DIM)
    hidden = residual[0].astype(jnp.float32) + jnp.dot(
        attended, out_proj, preferred_element_type=jnp.float32
    )
    mean_square = jnp.mean(hidden * hidden, axis=-1, keepdims=True)
    normed = (hidden * lax.rsqrt(mean_square + 1e-05) * norm_gain).astype(jnp.bfloat16)
    owners = lax.axis_size("exp")
    capacity = 3 * tok_count * TOP // (2 * owners)
    chosen = routes[0].reshape(-1)
    one_hot = (chosen[:, None] == jnp.arange(owners, dtype=jnp.int32)[None, :]).astype(jnp.int32)
    earlier = jnp.cumsum(one_hot, axis=0) - one_hot
    slot_index = jnp.sum(earlier * one_hot, axis=1)
    target = chosen * capacity + slot_index
    token_index = jnp.arange(tok_count * TOP, dtype=jnp.int32) // TOP
    slot_token = jnp.full((owners * capacity,), tok_count, jnp.int32).at[target].set(token_index)
    padded = jnp.concatenate([normed, jnp.zeros((1, normed.shape[1]), jnp.bfloat16)], axis=0)
    outgoing = padded[slot_token].reshape(owners, capacity, normed.shape[1])
    incoming = lax.all_to_all(outgoing, "exp", split_axis=0, concat_axis=0, tiled=True)
    sources, item_count, feature_width = incoming.shape
    flat_rows = incoming.reshape(sources * item_count, feature_width)
    gate_part = jnp.dot(flat_rows, w_gate[0], preferred_element_type=jnp.float32)
    up_part = jnp.dot(flat_rows, w_up[0], preferred_element_type=jnp.float32)
    activated = (jax.nn.silu(gate_part) * up_part).astype(jnp.bfloat16)
    produced = jnp.dot(activated, w_down[0], preferred_element_type=jnp.float32).astype(
        jnp.bfloat16
    )
    produced = produced.reshape(sources, item_count, feature_width)
    returned = lax.all_to_all(produced, "exp", split_axis=0, concat_axis=0, tiled=True)
    picked = (
        returned.reshape(owners * capacity, -1)[target]
        .astype(jnp.float32)
        .reshape(tok_count, TOP, -1)
    )
    mixture = jnp.sum(route_prob[0][:, :, None] * picked, axis=1)
    return (hidden + mixture).astype(jnp.bfloat16)[None]


def solution(mesh):
    placed = (
        P("exp", "ctx", None),
        P("exp", "ctx", None),
        P("exp", "ctx", None),
        P("exp", "ctx", None),
        P(),
        P(),
        P("exp", None, None),
        P("exp", None, None),
        P("exp", None, None),
        P("exp", "ctx", None),
        P("exp", "ctx", None),
    )
    return jax.shard_map(
        local, mesh=mesh, in_specs=placed, out_specs=P("exp", "ctx", None), check_vma=False
    )
```

profile of v0, /device:TPU:1, one launch (start us, length us, event | category | flops | bytes accessed | tf_op | source)
XLA Modules:
  0.0 383.2 jit_solution(7690073410518796440)
XLA Ops:
  6.5 1.3 copy.26
  7.8 1.1 copy.25
  8.9 1.3 pad_maximum_fusion
  10.2 0.8 copy.35
  11.2 0.9 copy.44
  12.2 0.7 broadcast_multiply_fusion
  13.1 0.6 reduce-window.6
  14.0 1.4 scatter_custom_fusion
  15.6 150.7 %all-gather.2.cloned.1.call-done = bf16[2,1536,1024]{2,0,1:T(2,128)(2,1)} async-done(((bf16[2,64,1024]{2,0,1:T(2,128)(2,1)}), bf16[2,1536,1024]{2,0,1:T(2,128)(2,1)}) %all-gather.2.cloned.1.call-update) | async-done | bytes 6291472 | tf_op jit(solution)/shard_map/all_gather | solution.py:51
  166.3 13.8 %fusion.57 = (bf16[1,1536,1024]{2,0,1:T(2,128)(2,1)}, bf16[1,1536,1024]{2,0,1:T(2,128)(2,1)}) fusion(bf16[2,1536,1024]{2,0,1:T(2,128)(2,1)} %all-gather.2.cloned.1.call-done), kind=kLoop, calls=%fused_computation.72 | loop fusion | bytes 12582912 | tf_op jit(solution)/shard_map/slice | solution.py:17
  180.1 15.3 %copy.41 = bf16[1,1536,1024]{1,2,0:T(8,128)(2,1)} copy(bf16[1,1536,1024]{2,0,1:T(2,128)(2,1)} %get-tuple-element.6) | data formatting | bytes 6291456
  195.4 15.3 %copy.40 = bf16[1,1536,1024]{1,2,0:T(8,128)(2,1)} copy(bf16[1,1536,1024]{2,0,1:T(2,128)(2,1)} %get-tuple-element.5) | data formatting | bytes 6291456
  210.7 2.7 fusion.58
  213.4 0.9 fusion.1
  214.3 1.0 copy-done.2
  215.3 1.3 fusion.32
  216.6 0.9 copy-done.1
  217.5 1.0 multiply_reduce_fusion.1
  218.7 3.1 gather_fusion
  221.8 3.6 reshape.115
  225.4 64.2 %all_to_all.10 = bf16[32,12,2048]{2,1,0:T(8,128)(2,1)} all-to-all(bf16[32,12,2048]{2,1,0:T(8,128)(2,1)} %reshape.115), channel_id=1, replica_groups=mesh['ctx'=24,'exp'=32] {'exp'}, dimensions={0} | all-to-all | bytes 3145728 | tf_op jit(solution)/shard_map/all_to_all | solution.py:72
  289.6 3.6 reshape.116
  293.3 3.9 %fusion.6 = f32[384,512]{1,0:T(8,128)} fusion(bf16[384,2048]{1,0:T(8,128)(2,1)} %reshape.116, bf16[1,2048,512]{2,1,0:T(8,128)(2,1)} %param.17), kind=kOutput, calls=%fused_computation.13 | convolution fusion | flops 805306368 | bytes 4456448 | tf_op jit(solution)/shard_map/dot_general | solution.py:75
  297.2 5.3 %convolution_convert_fusion = bf16[384,2048]{1,0:T(8,128)(2,1)} fusion(bf16[1,512,2048]{2,1,0:T(8,128)(2,1)S(1)} %copy-done, bf16[384,2048]{1,0:T(8,128)(2,1)} %reshape.116, bf16[1,2048,512]{2,1,0:T(8,128)(2,1)} %param.18, f32[384,512]{1,0:T(8,128)} %fusion.6), kind=kOutput, calls=%fused_computation.6 | convolution fusion | flops 1612578816 | bytes 8126464 | tf_op jit(solution)/shard_map/dot_general | solution.py:78
  302.5 3.6 reshape.117
  306.1 5.1 %all-to-all-start.1 = ((bf16[32,12,2048]{2,1,0:T(8,128)(2,1)}), bf16[32,12,2048]{2,1,0:T(8,128)(2,1)}, u32[]{:S(2)}, u32[]{:S(2)}) async-start(bf16[32,12,2048]{2,1,0:T(8,128)(2,1)} %reshape.117), calls=%async_computation.1 | async-start | bytes 4194304 | tf_op jit(solution)/shard_map/all_to_all | solution.py:82
  311.4 49.8 %all-to-all-done.1 = bf16[32,12,2048]{2,1,0:T(8,128)(2,1)} async-done(((bf16[32,12,2048]{2,1,0:T(8,128)(2,1)}), bf16[32,12,2048]{2,1,0:T(8,128)(2,1)}, u32[]{:S(2)}, u32[]{:S(2)}) %all-to-all-start.1) | async-done | bytes 1572896 | tf_op jit(solution)/shard_map/all_to_all | solution.py:82
  361.1 3.6 reshape.118
  364.7 4.9 %gather_fusion.1 = bf16[256,2048]{1,0:T(8,128)(2,1)} fusion(bf16[384,2048]{1,0:T(8,128)(2,1)} %reshape.118, s32[1024]{0:T(1024)S(1)} %pad_clamp_fusion), kind=kCustom, calls=%fused_computation.1 | custom fusion | bytes 2098176 | tf_op jit(solution)/shard_map/gather | solution.py:84
  369.7 2.7 reshape.120
  372.4 3.2 multiply_reduce_fusion
  375.6 0.8 fusion.43
  (34 shorter events, 1.2 us)
Async XLA Ops:
  6.5 290.7 %copy-start = (bf16[1,512,2048]{2,1,0:T(8,128)(2,1)S(1)}, bf16[1,512,2048]{2,1,0:T(8,128)(2,1)}, u32[]{:S(2)}) copy-start(bf16[1,512,2048]{2,1,0:T(8,128)(2,1)} %param.19) | copy-start | bytes 6291460
  6.5 159.7 %all-gather.2.cloned.1.call-start = ((), (), s32[]{:S(2)}) async-start(), calls=%async_computation.2 | async-start | bytes 6553600 | tf_op jit(solution)/shard_map/all_gather | solution.py:51
  213.4 1.9 copy-start.2
  215.3 2.2 copy-start.1
  215.3 2.2 copy-start.3
  217.5 1.0 copy-start.4
  302.5 8.7 %copy-start.5 = (f32[1,64,4]{1,2,0:T(4,128)S(1)}, f32[1,64,4]{1,2,0:T(4,128)}, u32[]{:S(2)}) copy-start(f32[1,64,4]{1,2,0:T(4,128)} %param.21) | copy-start | bytes 3076
  306.1 55.0 %all-to-all-start.1 = ((bf16[32,12,2048]{2,1,0:T(8,128)(2,1)}), bf16[32,12,2048]{2,1,0:T(8,128)(2,1)}, u32[]{:S(2)}, u32[]{:S(2)}) async-start(bf16[32,12,2048]{2,1,0:T(8,128)(2,1)} %reshape.117), calls=%async_computation.1 | async-start | bytes 4194304 | tf_op jit(solution)/shard_map/all_to_all | solution.py:82
Sparse Core Ops, SparseCore 0:
  10.9 155.3 all-gather.1
where the time goes:
time: 386 us; the launch traced here: 383 us
  waiting for transfers between devices  200 us (52%)
  local copies, waits for them, and re-layouts  77.8 us (20%)
  blocking collectives  64.2 us (17%)
  matrix products  14.3 us (4%)
  between operations  13.6 us (4%)
  other arithmetic  7.83 us (2%)
  starting transfers between devices  5.12 us (1%)
    all_gather x1, waiting for transfers between devices, local(): key_piece = lax.all_gather(stacked, 'ctx', axis=1, tiled=True)  151 us
    all_to_all x1, blocking collectives, local(): lax.all_to_all(outgoing, 'exp', split_axis=0, concat_axis=0, tiled=True)  64.2 us
    all_to_all x1, waiting for transfers between devices, local(): lax.all_to_all(produced, 'exp', split_axis=0, concat_axis=0, tiled=True)  49.8 us
    unnamed x18, local copies, waits for them, and re-layouts  36.6 us
    slice x1, local copies, waits for them, and re-layouts, attend_piece(): key_rows = key_piece[0].reshape(length, HEADS, HEAD_DIM)  13.8 us
  transfers between devices with their start and end apart: 2, of which 2 were waited for; matrix products, arithmetic and copies ran while one was open for 1% of the time, Pallas kernels for 0%

commit v1 on v0

v1 whole, which is shorter than its diff:
```python
import jax
import jax.numpy as jnp
from jax import lax
from jax.experimental import pallas as pl
from jax.experimental.pallas import tpu as pltpu
from jax.sharding import PartitionSpec as P

HEADS = 8
HEAD_DIM = 128
TOP = 4
TOK = 64
D = 2048
FFW = 512
N_CTX = 24
EXPERTS = 32
PARTS = N_CTX // HEADS
Q_ROWS = 24
CHUNK = 2 * TOK + Q_ROWS
GROUP = 6
MAIN = 8
REST = 4
WIDE = D + D // 2
SLOT_ROWS = EXPERTS * MAIN
REST_ROWS = EXPERTS * REST
f32 = jnp.float32
bf16 = jnp.bfloat16


def dot(a, b):
    return jnp.dot(a, b, preferred_element_type=f32)


def dot_first(a, b):
    return lax.dot_general(a, b, (((0,), (0,)), ((), ())), preferred_element_type=f32)


def part_rows(part):
    return min(Q_ROWS, TOK - part * Q_ROWS)


def pack_kernel(q_ref, k_ref, v_ref, o_ref):
    for head in range(HEADS):
        cols = slice(head * HEAD_DIM, (head + 1) * HEAD_DIM)
        for part in range(PARTS):
            rows = part_rows(part)
            chunk = head * PARTS + part
            o_ref[chunk, 0:TOK, :] = k_ref[:, cols]
            o_ref[chunk, TOK : 2 * TOK, :] = v_ref[:, cols]
            o_ref[chunk, 2 * TOK : 2 * TOK + rows, :] = q_ref[
                part * Q_ROWS : part * Q_ROWS + rows, cols
            ]
            if rows < Q_ROWS:
                o_ref[chunk, 2 * TOK + rows : CHUNK, :] = jnp.zeros((Q_ROWS - rows, HEAD_DIM), bf16)


def attend_kernel(part_ref, x_ref, o_ref):
    part = part_ref[0]
    factor = HEAD_DIM ** (-0.5)
    rows = GROUP * Q_ROWS
    span = GROUP * TOK
    row = lax.broadcasted_iota(jnp.int32, (rows, span), 0)
    block = jnp.zeros((rows, span), jnp.int32)
    for b in range(1, GROUP):
        block = block + (row >= b * Q_ROWS).astype(jnp.int32)
    query_pos = row + block * (TOK - Q_ROWS) + part * Q_ROWS
    allowed = lax.broadcasted_iota(jnp.int32, (rows, span), 1) <= query_pos
    for g in range(N_CTX // GROUP):
        lo = g * GROUP
        hi = lo + GROUP
        queries = x_ref[lo:hi, 2 * TOK : CHUNK, :].reshape(rows, HEAD_DIM)
        near_keys = x_ref[lo:hi, 0:TOK, :].reshape(span, HEAD_DIM)
        near_values = x_ref[lo:hi, TOK : 2 * TOK, :].reshape(span, HEAD_DIM)
        contract = (((1,), (1,)), ((), ()))
        near = lax.dot_general(queries, near_keys, contract, preferred_element_type=f32)
        near = jnp.where(allowed, near, -1e30)
        top = jnp.max(near, axis=1, keepdims=True)
        if g:
            far_keys = x_ref[0:lo, 0:TOK, :].reshape(lo * TOK, HEAD_DIM)
            far_values = x_ref[0:lo, TOK : 2 * TOK, :].reshape(lo * TOK, HEAD_DIM)
            far = lax.dot_general(queries, far_keys, contract, preferred_element_type=f32)
            top = jnp.maximum(top, jnp.max(far, axis=1, keepdims=True))
        near_exp = jnp.where(allowed, jnp.exp((near - top) * factor), 0.0)
        total = jnp.sum(near_exp, axis=1, keepdims=True)
        acc = dot(near_exp.astype(bf16), near_values)
        if g:
            far_exp = jnp.exp((far - top) * factor)
            total = total + jnp.sum(far_exp, axis=1, keepdims=True)
            acc = acc + dot(far_exp.astype(bf16), far_values)
        o_ref[lo:hi] = (acc / total).astype(bf16).reshape(GROUP, Q_ROWS, HEAD_DIM)


def slot_values(routes):
    expert = lax.broadcasted_iota(jnp.int32, (EXPERTS, TOK), 0)
    named = jnp.zeros((EXPERTS, TOK), f32)
    for k in range(TOP):
        named = named + (routes[k : k + 1, :] == expert).astype(f32)
    earlier = (
        lax.broadcasted_iota(jnp.int32, (TOK, TOK), 0)
        < lax.broadcasted_iota(jnp.int32, (TOK, TOK), 1)
    ).astype(bf16)
    return named * (1.0 + dot(named.astype(bf16), earlier))


def spread():
    row = lax.broadcasted_iota(jnp.int32, (SLOT_ROWS, EXPERTS), 0)
    return ((row >> 3) == lax.broadcasted_iota(jnp.int32, (SLOT_ROWS, EXPERTS), 1)).astype(bf16)


def slot_masks(routes):
    value = dot(spread(), slot_values(routes).astype(bf16))
    row = lax.broadcasted_iota(jnp.int32, (SLOT_ROWS, TOK), 0)
    main = value == ((row & 7) + 1).astype(f32)
    rest = value == ((row & 3) + 1 + MAIN).astype(f32)
    low = (row & 7) < REST
    return main, rest & low, rest & (~low)


def project_kernel(a_ref, residual_ref, w_ref, gain_ref, routes_ref, hidden_ref, o_ref, rows_ref):
    for head in range(HEADS):
        cols = slice(head * HEAD_DIM, (head + 1) * HEAD_DIM)
        for part in range(PARTS):
            rows = part_rows(part)
            rows_ref[part * Q_ROWS : part * Q_ROWS + rows, cols] = a_ref[
                head * PARTS + part, 0:rows, :
            ]
    hidden = residual_ref[...].astype(f32) + dot(rows_ref[...], w_ref[...])
    hidden_ref[...] = hidden
    mean_square = jnp.mean(hidden * hidden, axis=-1, keepdims=True)
    normed = (hidden * lax.rsqrt(mean_square + 1e-05) * gain_ref[...]).astype(bf16)
    main, low, high = slot_masks(routes_ref[...])
    o_ref[:, 0:D] = dot(main.astype(bf16), normed).astype(bf16)
    o_ref[:, D:WIDE] = (
        dot(low.astype(bf16), normed[:, 0 : D // 2]) + dot(high.astype(bf16), normed[:, D // 2 : D])
    ).astype(bf16)


def picker(high):
    row = lax.broadcasted_iota(jnp.int32, (REST_ROWS, SLOT_ROWS), 0)
    col = lax.broadcasted_iota(jnp.int32, (REST_ROWS, SLOT_ROWS), 1)
    return (col == (row >> 2) * MAIN + (row & 3) + (REST if high else 0)).astype(bf16)


def expert_kernel(x_ref, gate_ref, up_ref, down_ref, o_ref, rows_ref):
    low, high = picker(False), picker(True)
    rows_ref[0:SLOT_ROWS, :] = x_ref[:, 0:D]
    rows_ref[SLOT_ROWS:, 0 : D // 2] = dot(low, x_ref[:, D:WIDE]).astype(bf16)
    rows_ref[SLOT_ROWS:, D // 2 : D] = dot(high, x_ref[:, D:WIDE]).astype(bf16)
    gate = dot(rows_ref[...], gate_ref[...])
    up = dot(rows_ref[...], up_ref[...])
    act = (gate / (1.0 + jnp.exp(-gate)) * up).astype(bf16)
    made = dot(act, down_ref[...]).astype(bf16)
    o_ref[:, 0:D] = made[0:SLOT_ROWS]
    o_ref[:, D:WIDE] = (
        dot_first(low, made[SLOT_ROWS:, 0 : D // 2]) + dot_first(high, made[SLOT_ROWS:, D // 2 : D])
    ).astype(bf16)


def mix_kernel(y_ref, hidden_ref, routes_ref, prob_ref, o_ref):
    routes = routes_ref[...]
    main, low, high = slot_masks(routes)
    expert = lax.broadcasted_iota(jnp.int32, (EXPERTS, TOK), 0)
    prob = jnp.zeros((EXPERTS, TOK), f32)
    for k in range(TOP):
        prob = prob + jnp.where(routes[k : k + 1, :] == expert, prob_ref[k : k + 1, :], 0.0)
    mixed = hidden_ref[...]
    rest = y_ref[:, D:WIDE]
    first = jnp.zeros((TOK, D // 2), f32)
    second = jnp.zeros((TOK, D // 2), f32)
    for _ in range(3):
        term = prob.astype(bf16)
        prob = prob - term.astype(f32)
        wide = dot(spread(), term)
        mixed = mixed + dot_first(jnp.where(main, wide, 0.0).astype(bf16), y_ref[:, 0:D])
        first = first + dot_first(jnp.where(low, wide, 0.0).astype(bf16), rest)
        second = second + dot_first(jnp.where(high, wide, 0.0).astype(bf16), rest)
    o_ref[:, 0 : D // 2] = (mixed[:, 0 : D // 2] + first).astype(bf16)
    o_ref[:, D // 2 : D] = (mixed[:, D // 2 : D] + second).astype(bf16)


def call(kernel, name, outs, *args, scratch=(), smem=0):
    vmem = pl.BlockSpec(memory_space=pltpu.VMEM)
    specs = [pl.BlockSpec(memory_space=pltpu.SMEM)] * smem + [vmem] * (len(args) - smem)
    many = isinstance(outs, list)
    return pl.pallas_call(
        kernel,
        out_shape=outs,
        in_specs=specs,
        out_specs=[vmem] * len(outs) if many else vmem,
        scratch_shapes=scratch,
        name=name,
        compiler_params=pltpu.CompilerParams(vmem_limit_bytes=56 * 1024 * 1024),
    )(*args)


def exchange(x, axis):
    return lax.all_to_all(x, axis, split_axis=0, concat_axis=0, tiled=True)


def local(
    queries, keys, values, residual, out_proj, norm_gain, w_gate, w_up, w_down, routes, route_prob
):
    shape = jax.ShapeDtypeStruct
    routes_t = routes[0].T
    prob_t = route_prob[0].T
    part = (lax.axis_index("ctx") % PARTS).astype(jnp.int32).reshape(1)
    packed = call(
        pack_kernel, "pack", shape((N_CTX, CHUNK, HEAD_DIM), bf16), queries[0], keys[0], values[0]
    )
    gathered = exchange(packed, "ctx")
    attended = call(
        attend_kernel, "attend", shape((N_CTX, Q_ROWS, HEAD_DIM), bf16), part, gathered, smem=1
    )
    mine = exchange(attended, "ctx")
    hidden, outgoing = call(
        project_kernel,
        "project",
        [shape((TOK, D), f32), shape((SLOT_ROWS, WIDE), bf16)],
        mine,
        residual[0],
        out_proj,
        norm_gain.reshape(1, D),
        routes_t,
        scratch=[pltpu.VMEM((TOK, HEADS * HEAD_DIM), bf16)],
    )
    incoming = exchange(outgoing.reshape(EXPERTS, MAIN, WIDE), "exp").reshape(SLOT_ROWS, WIDE)
    made = call(
        expert_kernel,
        "experts",
        shape((SLOT_ROWS, WIDE), bf16),
        incoming,
        w_gate[0],
        w_up[0],
        w_down[0],
        scratch=[pltpu.VMEM((SLOT_ROWS + REST_ROWS, D), bf16)],
    )
    returned = exchange(made.reshape(EXPERTS, MAIN, WIDE), "exp").reshape(SLOT_ROWS, WIDE)
    return call(mix_kernel, "mix", shape((TOK, D), bf16), returned, hidden, routes_t, prob_t)[None]


def solution(mesh):
    placed = (
        P("exp", "ctx", None),
        P("exp", "ctx", None),
        P("exp", "ctx", None),
        P("exp", "ctx", None),
        P(),
        P(),
        P("exp", None, None),
        P("exp", None, None),
        P("exp", None, None),
        P("exp", "ctx", None),
        P("exp", "ctx", None),
    )
    return jax.shard_map(
        local, mesh=mesh, in_specs=placed, out_specs=P("exp", "ctx", None), check_vma=False
    )
```

time: 386 us -> 192 us (0.50)
  waiting for transfers between devices: 200 us -> 35.1 us
  local copies, waits for them, and re-layouts: 77.8 us -> 0.93 us
  blocking collectives: 64.2 us -> 115 us
  Pallas kernels: 0 us -> 22.7 us
  matrix products: 14.3 us -> 0 us
  between operations: 13.6 us -> 0.04 us
  starting transfers between devices: 5.12 us -> 18.4 us
  other arithmetic: 7.83 us -> 0 us
    all_gather x1 -> x0, waiting for transfers between devices: 151 us -> none  [local(): key_piece = lax.all_gather(stacked, 'ctx', axis=1, tiled=True)]
    all_to_all x1 -> x3, blocking collectives: 64.2 us -> 115 us  [exchange(): return lax.all_to_all(x, axis, split_axis=0, concat_axis=0, tiled=True)]
    unnamed x18 -> x2, local copies, waits for them, and re-layouts: 36.6 us -> 0.93 us
    pallas_call x0 -> x5, Pallas kernels: none -> 22.7 us  [call(): pl.pallas_call(kernel, out_shape=outs, in_specs=specs, out_specs=[vmem] *...]
    all_to_all x1, waiting for transfers between devices: 49.8 us -> 35.1 us  [exchange(): return lax.all_to_all(x, axis, split_axis=0, concat_axis=0, tiled=True)]
    reshape x4 -> x0, local copies, waits for them, and re-layouts: 14.5 us -> none  [the longest x1 3.64 us: local(): flat_rows = incoming.reshape(sources * item_count, feature_width)]
    dot_general x5 -> x0, matrix products: 14.3 us -> none  [the longest x1 5.32 us: local(): jnp.dot(activated, w_down[0], preferred_element_type=jnp.float32)]
    slice x2 -> x0, local copies, waits for them, and re-layouts: 14 us -> none  [the longest x1 13.8 us: attend_piece(): key_rows = key_piece[0].reshape(length, HEADS, HEAD_DIM)]
  transfers between devices with their start and end apart: 2 -> 1, of which waited for: 2 -> 1; matrix products, arithmetic and copies ran while one was open for 1% -> 0% of each run, Pallas kernels for 0% -> 0%
where the time goes in v1:
time: 192 us
  blocking collectives  115 us (60%)
  waiting for transfers between devices  35.1 us (18%)
  Pallas kernels  22.7 us (12%)
  starting transfers between devices  18.4 us (10%)
    all_to_all x3, blocking collectives, exchange(): return lax.all_to_all(x, axis, split_axis=0, concat_axis=0, tiled=True)  115 us
    all_to_all x1, waiting for transfers between devices, exchange(): return lax.all_to_all(x, axis, split_axis=0, concat_axis=0, tiled=True)  35.1 us
    pallas_call x5, Pallas kernels, call(): pl.pallas_call(kernel, out_shape=outs, in_specs=specs, out_specs=[vmem] *...  22.7 us
    all_to_all x1, starting transfers between devices, exchange(): return lax.all_to_all(x, axis, split_axis=0, concat_axis=0, tiled=True)  18.4 us
  transfers between devices with their start and end apart: 1, of which 1 were waited for; matrix products, arithmetic and copies ran while one was open for 0% of the time, Pallas kernels for 0%

profile of v1, /device:TPU:1, one launch (start us, length us, event | category | flops | bytes accessed | tf_op | source)
XLA Modules:
  0.0 191.7 jit_solution(3912703195712862126)
XLA Ops:
  0.0 2.1 %pack.1 = bf16[24,152,128]{2,1,0:T(8,128)(2,1)} custom-call(bf16[64,1024]{1,0:T(8,128)(2,1)} %bitcast.28, bf16[64,1024]{1,0:T(8,128)(2,1)} %bitcast.29, bf16[64,1024]{1,0:T(8,128)(2,1)} %bitcast.30), custom_call_target="tpu_custom_call" | custom-call | tf_op jit(solution)/shard_map/pack/pallas_call | solution.py:184
  2.1 18.4 %all-to-all-start = ((bf16[24,152,128]{2,1,0:T(8,128)(2,1)}), bf16[24,152,128]{2,1,0:T(8,128)(2,1)S(1)}, u32[]{:S(2)}, u32[]{:S(2)}) async-start(bf16[24,152,128]{2,1,0:T(8,128)(2,1)} %pack.1), calls=%async_computation | async-start | bytes 1867776 | tf_op jit(solution)/shard_map/all_to_all | solution.py:196
  20.5 35.1 %all-to-all-done.x_ref = bf16[24,152,128]{2,1,0:T(8,128)(2,1)S(1)} async-done(((bf16[24,152,128]{2,1,0:T(8,128)(2,1)}), bf16[24,152,128]{2,1,0:T(8,128)(2,1)S(1)}, u32[]{:S(2)}, u32[]{:S(2)}) %all-to-all-start) | async-done | bytes 933920 | tf_op jit(solution)/shard_map/all_to_all | solution.py:196
  55.6 0.0 copy-start
  55.6 0.9 copy-done
  56.5 3.6 %attend.1 = bf16[24,24,128]{2,1,0:T(8,128)(2,1)} custom-call(s32[1]{0:T(128)} %bitcast.part_ref, bf16[24,152,128]{2,1,0:T(8,128)(2,1)} %copy-done), custom_call_target="tpu_custom_call" | custom-call | tf_op jit(solution)/shard_map/attend/pallas_call | solution.py:184
  60.1 20.1 %all_to_all.20.a_ref = bf16[24,24,128]{2,1,0:T(8,128)(2,1)} all-to-all(bf16[24,24,128]{2,1,0:T(8,128)(2,1)} %attend.1), channel_id=1, replica_groups=mesh['ctx'=24,'exp'=32] {'ctx'}, dimensions={0} | all-to-all | bytes 294912 | tf_op jit(solution)/shard_map/all_to_all | solution.py:196
  80.3 5.2 %project.1 = (f32[64,2048]{1,0:T(8,128)}, bf16[256,3072]{1,0:T(8,128)(2,1)}) custom-call(bf16[24,24,128]{2,1,0:T(8,128)(2,1)} %all_to_all.20.a_ref, bf16[64,2048]{1,0:T(8,128)(2,1)} %bitcast.27, bf16[1024,2048]{1,0:T(8,128)(2,1)} %w_ref.1, f32[1,2048]{1,0:T(1,128)} %bitcast.31, s32[4,64]{1,0:T(4,128)} %bitcast.32), custom_call_target="tpu_custom_call" | custom-call | tf_op jit(solution)/shard_map/project/pallas_call | solution.py:184
  85.5 49.7 %all_to_all.21 = bf16[32,8,3072]{2,1,0:T(8,128)(2,1)} all-to-all(bf16[32,8,3072]{2,1,0:T(8,128)(2,1)} %bitcast.26), channel_id=1, replica_groups=mesh['ctx'=24,'exp'=32] {'exp'}, dimensions={0} | all-to-all | bytes 3145728 | tf_op jit(solution)/shard_map/all_to_all | solution.py:196
  135.2 7.6 %experts.1 = bf16[256,3072]{1,0:T(8,128)(2,1)} custom-call(bf16[256,3072]{1,0:T(8,128)(2,1)} %bitcast.21, bf16[2048,512]{1,0:T(8,128)(2,1)} %bitcast.23, bf16[2048,512]{1,0:T(8,128)(2,1)} %bitcast.24, bf16[512,2048]{1,0:T(8,128)(2,1)} %bitcast.25), custom_call_target="tpu_custom_call" | custom-call | tf_op jit(solution)/shard_map/experts/pallas_call | solution.py:184
  142.8 44.7 %all_to_all.22 = bf16[32,8,3072]{2,1,0:T(8,128)(2,1)} all-to-all(bf16[32,8,3072]{2,1,0:T(8,128)(2,1)} %bitcast.22), channel_id=1, replica_groups=mesh['ctx'=24,'exp'=32] {'exp'}, dimensions={0} | all-to-all | bytes 3145728 | tf_op jit(solution)/shard_map/all_to_all | solution.py:196
  187.5 4.2 %mix.1 = bf16[64,2048]{1,0:T(8,128)(2,1)} custom-call(bf16[256,3072]{1,0:T(8,128)(2,1)} %bitcast.20, f32[64,2048]{1,0:T(8,128)} %get-tuple-element.8.hidden_ref, s32[4,64]{1,0:T(4,128)} %bitcast.33, f32[4,64]{1,0:T(4,128)} %bitcast.34), custom_call_target="tpu_custom_call" | custom-call | tf_op jit(solution)/shard_map/mix/pallas_call | solution.py:184
Async XLA Ops:
  2.1 53.5 %all-to-all-start = ((bf16[24,152,128]{2,1,0:T(8,128)(2,1)}), bf16[24,152,128]{2,1,0:T(8,128)(2,1)S(1)}, u32[]{:S(2)}, u32[]{:S(2)}) async-start(bf16[24,152,128]{2,1,0:T(8,128)(2,1)} %pack.1), calls=%async_computation | async-start | bytes 1867776 | tf_op jit(solution)/shard_map/all_to_all | solution.py:196
  55.6 0.9 copy-start

commit v2 on v1

v2 whole, which is shorter than its diff:
```python
import jax
import jax.numpy as jnp
from jax import lax
from jax.experimental import pallas as pl
from jax.experimental.pallas import tpu as pltpu
from jax.sharding import PartitionSpec as P

HEADS = 8
HEAD_DIM = 128
TOP = 4
TOK = 64
D = 2048
FFW = 512
N_CTX = 24
EXPERTS = 32
PARTS = N_CTX // HEADS
Q_ROWS = 24
CHUNK = 2 * TOK + Q_ROWS
GROUP = 6
MAIN = 8
REST = 4
HALF = D // 2
WIDE = D + HALF
SLOT_ROWS = EXPERTS * MAIN
REST_ROWS = EXPERTS * REST
f32 = jnp.float32
bf16 = jnp.bfloat16


def dot(a, b):
    return jnp.dot(a, b, preferred_element_type=f32)


def dot_first(a, b):
    return lax.dot_general(a, b, (((0,), (0,)), ((), ())), preferred_element_type=f32)


def dot_last(a, b):
    return lax.dot_general(a, b, (((1,), (1,)), ((), ())), preferred_element_type=f32)


def part_rows(part):
    return min(Q_ROWS, TOK - part * Q_ROWS)


def pack_kernel(q_ref, k_ref, v_ref, o_ref):
    for head in range(HEADS):
        cols = slice(head * HEAD_DIM, (head + 1) * HEAD_DIM)
        for part in range(PARTS):
            rows = part_rows(part)
            chunk = head * PARTS + part
            o_ref[chunk, 0:TOK, :] = k_ref[:, cols]
            o_ref[chunk, TOK : 2 * TOK, :] = v_ref[:, cols]
            o_ref[chunk, 2 * TOK : 2 * TOK + rows, :] = q_ref[
                part * Q_ROWS : part * Q_ROWS + rows, cols
            ]
            if rows < Q_ROWS:
                o_ref[chunk, 2 * TOK + rows : CHUNK, :] = jnp.zeros((Q_ROWS - rows, HEAD_DIM), bf16)


def attend_kernel(part_ref, x_ref, o_ref):
    factor = HEAD_DIM ** (-0.5) * 1.4426950408889634
    rows = GROUP * Q_ROWS
    span = GROUP * TOK
    row = lax.broadcasted_iota(jnp.int32, (rows, span), 0)
    block = jnp.zeros((rows, span), jnp.int32)
    for b in range(1, GROUP):
        block = block + (row >= b * Q_ROWS).astype(jnp.int32)
    query_pos = row + block * (TOK - Q_ROWS) + part_ref[0] * Q_ROWS
    allowed = lax.broadcasted_iota(jnp.int32, (rows, span), 1) <= query_pos
    for g in range(N_CTX // GROUP):
        lo = g * GROUP
        hi = lo + GROUP
        queries = x_ref[lo:hi, 2 * TOK : CHUNK, :].reshape(rows, HEAD_DIM)
        near_keys = x_ref[lo:hi, 0:TOK, :].reshape(span, HEAD_DIM)
        near_values = x_ref[lo:hi, TOK : 2 * TOK, :].reshape(span, HEAD_DIM)
        near = jnp.where(allowed, dot_last(queries, near_keys), -1e30)
        top = jnp.max(near, axis=1, keepdims=True)
        if g:
            far_keys = x_ref[0:lo, 0:TOK, :].reshape(lo * TOK, HEAD_DIM)
            far_values = x_ref[0:lo, TOK : 2 * TOK, :].reshape(lo * TOK, HEAD_DIM)
            far = dot_last(queries, far_keys)
            top = jnp.maximum(top, jnp.max(far, axis=1, keepdims=True))
        near_exp = jnp.exp2((near - top) * factor)
        total = jnp.sum(near_exp, axis=1, keepdims=True)
        acc = dot(near_exp.astype(bf16), near_values)
        if g:
            far_exp = jnp.exp2((far - top) * factor)
            total = total + jnp.sum(far_exp, axis=1, keepdims=True)
            acc = acc + dot(far_exp.astype(bf16), far_values)
        o_ref[lo:hi] = (acc / total).astype(bf16).reshape(GROUP, Q_ROWS, HEAD_DIM)


def plan_kernel(routes_ref, prob_ref, *outs):
    routes = routes_ref[...]
    expert = lax.broadcasted_iota(jnp.int32, (EXPERTS, TOK), 0)
    named = jnp.zeros((EXPERTS, TOK), f32)
    prob = jnp.zeros((EXPERTS, TOK), f32)
    for k in range(TOP):
        here = routes[k : k + 1, :] == expert
        named = named + here.astype(f32)
        prob = prob + jnp.where(here, prob_ref[k : k + 1, :], 0.0)
    earlier = (
        lax.broadcasted_iota(jnp.int32, (TOK, TOK), 0)
        < lax.broadcasted_iota(jnp.int32, (TOK, TOK), 1)
    ).astype(bf16)
    slot = named * (1.0 + dot(named.astype(bf16), earlier))
    spread = (
        (lax.broadcasted_iota(jnp.int32, (SLOT_ROWS, EXPERTS), 0) >> 3)
        == lax.broadcasted_iota(jnp.int32, (SLOT_ROWS, EXPERTS), 1)
    ).astype(bf16)
    value = dot(spread, slot.astype(bf16))
    row = lax.broadcasted_iota(jnp.int32, (SLOT_ROWS, TOK), 0)
    main = value == ((row & 7) + 1).astype(f32)
    rest = value == ((row & 3) + 1 + MAIN).astype(f32)
    low = (row & 7) < REST
    masks = (main, rest & low, rest & (~low))
    for mask, out in zip(masks, outs[:3]):
        out[...] = mask.astype(bf16)
    for term in range(3):
        part = prob.astype(bf16)
        prob = prob - part.astype(f32)
        wide = dot(spread, part)
        for mask, out in zip(masks, outs[3:]):
            out[term] = jnp.where(mask, wide, 0.0).astype(bf16)


def project_kernel(
    a_ref, residual_ref, w_ref, gain_ref, m_ref, l_ref, h_ref, hidden_ref, o_ref, rows_ref
):
    for head in range(HEADS):
        cols = slice(head * HEAD_DIM, (head + 1) * HEAD_DIM)
        for part in range(PARTS):
            rows = part_rows(part)
            rows_ref[part * Q_ROWS : part * Q_ROWS + rows, cols] = a_ref[
                head * PARTS + part, 0:rows, :
            ]
    hidden = residual_ref[...].astype(f32) + dot(rows_ref[...], w_ref[...])
    hidden_ref[...] = hidden
    mean_square = jnp.mean(hidden * hidden, axis=-1, keepdims=True)
    normed = (hidden * lax.rsqrt(mean_square + 1e-05) * gain_ref[...]).astype(bf16)
    o_ref[:, 0:D] = dot(m_ref[...], normed).astype(bf16)
    o_ref[:, D:WIDE] = (
        dot(l_ref[...], normed[:, 0:HALF]) + dot(h_ref[...], normed[:, HALF:D])
    ).astype(bf16)


def picker(high):
    row = lax.broadcasted_iota(jnp.int32, (REST_ROWS, SLOT_ROWS), 0)
    col = lax.broadcasted_iota(jnp.int32, (REST_ROWS, SLOT_ROWS), 1)
    return (col == (row >> 2) * MAIN + (row & 3) + (REST if high else 0)).astype(bf16)


def expert_kernel(x_ref, gate_ref, up_ref, down_ref, o_ref, rows_ref):
    low, high = picker(False), picker(True)
    rows_ref[0:SLOT_ROWS, :] = x_ref[:, 0:D]
    rows_ref[SLOT_ROWS:, 0 : HALF] = dot(low, x_ref[:, D:WIDE]).astype(bf16)
    rows_ref[SLOT_ROWS:, HALF : D] = dot(high, x_ref[:, D:WIDE]).astype(bf16)
    gate = dot(rows_ref[...], gate_ref[...])
    up = dot(rows_ref[...], up_ref[...])
    act = (gate / (1.0 + jnp.exp(-gate)) * up).astype(bf16)
    made = dot(act, down_ref[...]).astype(bf16)
    o_ref[:, 0:D] = made[0:SLOT_ROWS]
    o_ref[:, D:WIDE] = (
        dot_first(low, made[SLOT_ROWS:, 0 : HALF]) + dot_first(high, made[SLOT_ROWS:, HALF : D])
    ).astype(bf16)


def mix_kernel(y_ref, hidden_ref, m_ref, l_ref, h_ref, o_ref):
    total = hidden_ref[...]
    rest = y_ref[:, D:WIDE]
    first = jnp.zeros((TOK, HALF), f32)
    second = jnp.zeros((TOK, HALF), f32)
    for term in range(3):
        total = total + dot_first(m_ref[term], y_ref[:, 0:D])
        first = first + dot_first(l_ref[term], rest)
        second = second + dot_first(h_ref[term], rest)
    o_ref[:, 0:HALF] = (total[:, 0:HALF] + first).astype(bf16)
    o_ref[:, HALF:D] = (total[:, HALF:D] + second).astype(bf16)


def call(kernel, name, outs, *args, scratch=(), smem=0, mib=16):
    vmem = pl.BlockSpec(memory_space=pltpu.VMEM)
    specs = [pl.BlockSpec(memory_space=pltpu.SMEM)] * smem + [vmem] * (len(args) - smem)
    many = isinstance(outs, list)
    return pl.pallas_call(
        kernel,
        out_shape=outs,
        in_specs=specs,
        out_specs=[vmem] * len(outs) if many else vmem,
        scratch_shapes=scratch,
        name=name,
        compiler_params=pltpu.CompilerParams(vmem_limit_bytes=mib * 1024 * 1024),
    )(*args)


def of(*dims, dtype=bf16):
    return jax.ShapeDtypeStruct(dims, dtype)


def pack(queries, keys, values):
    return call(pack_kernel, "pack", of(N_CTX, CHUNK, HEAD_DIM), queries, keys, values, mib=8)


def attend(part, gathered):
    return call(attend_kernel, "attend", of(N_CTX, Q_ROWS, HEAD_DIM), part, gathered, smem=1)


def plan(routes, prob):
    outs = [of(SLOT_ROWS, TOK)] * 3 + [of(3, SLOT_ROWS, TOK)] * 3
    made = call(plan_kernel, "plan", outs, routes.T, prob.T, mib=8)
    return made[:3], made[3:]


def project(attended, residual, out_proj, norm_gain, masks):
    outs = [of(TOK, D, dtype=f32), of(SLOT_ROWS, WIDE)]
    scratch = [pltpu.VMEM((TOK, HEADS * HEAD_DIM), bf16)]
    gain = norm_gain.reshape(1, D)
    return call(
        project_kernel, "project", outs, attended, residual, out_proj, gain, *masks, scratch=scratch
    )


def experts(rows, w_gate, w_up, w_down):
    scratch = [pltpu.VMEM((SLOT_ROWS + REST_ROWS, D), bf16)]
    outs = of(SLOT_ROWS, WIDE)
    return call(
        expert_kernel, "experts", outs, rows, w_gate, w_up, w_down, scratch=scratch, mib=24
    )


def mix(rows, hidden, probs):
    return call(mix_kernel, "mix", of(TOK, D), rows, hidden, *probs)


def exchange(x, axis):
    return lax.all_to_all(x, axis, split_axis=0, concat_axis=0, tiled=True)


def slots_exchange(x):
    return exchange(x.reshape(EXPERTS, MAIN, WIDE), "exp").reshape(SLOT_ROWS, WIDE)


def local(
    queries, keys, values, residual, out_proj, norm_gain, w_gate, w_up, w_down, routes, route_prob
):
    part = (lax.axis_index("ctx") % PARTS).astype(jnp.int32).reshape(1)
    gathered = exchange(pack(queries[0], keys[0], values[0]), "ctx")
    masks, probs = plan(routes[0], route_prob[0])
    attended = exchange(attend(part, gathered), "ctx")
    hidden, rows = project(attended, residual[0], out_proj, norm_gain, masks)
    rows = slots_exchange(rows)
    rows = slots_exchange(experts(rows, w_gate[0], w_up[0], w_down[0]))
    return mix(rows, hidden, probs)[None]


def solution(mesh):
    placed = (
        P("exp", "ctx", None),
        P("exp", "ctx", None),
        P("exp", "ctx", None),
        P("exp", "ctx", None),
        P(),
        P(),
        P("exp", None, None),
        P("exp", None, None),
        P("exp", None, None),
        P("exp", "ctx", None),
        P("exp", "ctx", None),
    )
    return jax.shard_map(
        local, mesh=mesh, in_specs=placed, out_specs=P("exp", "ctx", None), check_vma=False
    )
```

time: 192 us -> 182 us (0.948)
  blocking collectives: 115 us -> 93 us
  Pallas kernels: 22.7 us -> 10.6 us
  waiting for transfers between devices: 35.1 us -> 46.7 us
  starting transfers between devices: 18.4 us -> 26.3 us
  local copies, waits for them, and re-layouts: 0.93 us -> 4.93 us
    all_to_all x3 -> x2, blocking collectives: 115 us -> 93 us  [exchange(): return lax.all_to_all(x, axis, split_axis=0, concat_axis=0, tiled=True)]
    pallas_call x5 -> x6, Pallas kernels: 22.7 us -> 10.6 us  [call(): pl.pallas_call(kernel, out_shape=outs, in_specs=specs, out_specs=[vmem] *...]
    all_to_all x1 -> x2, waiting for transfers between devices: 35.1 us -> 46.7 us  [exchange(): return lax.all_to_all(x, axis, split_axis=0, concat_axis=0, tiled=True)]
    all_to_all x1 -> x2, starting transfers between devices: 18.4 us -> 26.3 us  [exchange(): return lax.all_to_all(x, axis, split_axis=0, concat_axis=0, tiled=True)]
    unnamed x2 -> x22, local copies, waits for them, and re-layouts: 0.93 us -> 4.93 us
  transfers between devices with their start and end apart: 1 -> 2, of which waited for: 1 -> 2; matrix products, arithmetic and copies ran while one was open for 0% -> 0% of each run, Pallas kernels for 0% -> 0%
where the time goes in v2:
time: 182 us
  blocking collectives  93 us (51%)
  waiting for transfers between devices  46.7 us (26%)
  starting transfers between devices  26.3 us (14%)
  Pallas kernels  10.6 us (6%)
  local copies, waits for them, and re-layouts  4.93 us (3%)
    all_to_all x2, blocking collectives, exchange(): return lax.all_to_all(x, axis, split_axis=0, concat_axis=0, tiled=True)  93 us
    all_to_all x2, waiting for transfers between devices, exchange(): return lax.all_to_all(x, axis, split_axis=0, concat_axis=0, tiled=True)  46.7 us
    all_to_all x2, starting transfers between devices, exchange(): return lax.all_to_all(x, axis, split_axis=0, concat_axis=0, tiled=True)  26.3 us
    pallas_call x6, Pallas kernels, call(): pl.pallas_call(kernel, out_shape=outs, in_specs=specs, out_specs=[vmem] *...  10.6 us
    unnamed x22, local copies, waits for them, and re-layouts  4.93 us
  transfers between devices with their start and end apart: 2, of which 2 were waited for; matrix products, arithmetic and copies ran while one was open for 0% of the time, Pallas kernels for 0%

profile of v2, /device:TPU:1, one launch (start us, length us, event | category | flops | bytes accessed | tf_op | source)
XLA Modules:
  0.0 181.6 jit_solution(12848206688586331731)
XLA Ops:
  0.0 0.0 copy-start.5
  0.0 0.9 copy-done.5
  0.9 0.0 copy-start.6
  0.9 0.9 copy-done.6
  1.8 0.0 copy-start.7
  1.8 0.9 copy-done.7
  2.7 0.0 copy-start.9
  2.7 0.0 copy-start.10
  2.7 0.0 copy-start.4
  2.7 0.0 copy-start.8
  2.7 1.0 pack.1
  3.8 18.4 %all-to-all-start = ((bf16[24,152,128]{2,1,0:T(8,128)(2,1)}), bf16[24,152,128]{2,1,0:T(8,128)(2,1)S(1)}, u32[]{:S(2)}, u32[]{:S(2)}) async-start(bf16[24,152,128]{2,1,0:T(8,128)(2,1)} %pack.1), calls=%async_computation | async-start | bytes 1867776 | tf_op jit(solution)/shard_map/all_to_all | solution.py:237
  22.2 35.1 %all-to-all-done.x_ref = bf16[24,152,128]{2,1,0:T(8,128)(2,1)S(1)} async-done(((bf16[24,152,128]{2,1,0:T(8,128)(2,1)}), bf16[24,152,128]{2,1,0:T(8,128)(2,1)S(1)}, u32[]{:S(2)}, u32[]{:S(2)}) %all-to-all-start) | async-done | bytes 933920 | tf_op jit(solution)/shard_map/all_to_all | solution.py:237
  57.3 2.4 %attend.1 = bf16[24,24,128]{2,1,0:T(8,128)(2,1)} custom-call(s32[1]{0:T(128)} %bitcast.part_ref, bf16[24,152,128]{2,1,0:T(8,128)(2,1)S(1)} %all-to-all-done.x_ref), custom_call_target="tpu_custom_call" | custom-call | tf_op jit(solution)/shard_map/attend/pallas_call | solution.py:186
  59.6 8.0 %all-to-all-start.1 = ((bf16[24,24,128]{2,1,0:T(8,128)(2,1)}), bf16[24,24,128]{2,1,0:T(8,128)(2,1)S(1)}, u32[]{:S(2)}, u32[]{:S(2)}) async-start(bf16[24,24,128]{2,1,0:T(8,128)(2,1)} %attend.1), calls=%async_computation.1 | async-start | bytes 294912 | tf_op jit(solution)/shard_map/all_to_all | solution.py:237
  67.6 0.0 copy-done.9
  67.6 0.0 copy-done.10
  67.6 0.4 plan.1
  68.1 11.6 %all-to-all-done.1.a_ref = bf16[24,24,128]{2,1,0:T(8,128)(2,1)S(1)} async-done(((bf16[24,24,128]{2,1,0:T(8,128)(2,1)}), bf16[24,24,128]{2,1,0:T(8,128)(2,1)S(1)}, u32[]{:S(2)}, u32[]{:S(2)}) %all-to-all-start.1) | async-done | bytes 147488 | tf_op jit(solution)/shard_map/all_to_all | solution.py:237
  79.7 0.0 copy-done.4
  79.7 0.0 copy-done.8
  79.7 0.0 copy-start
  79.7 2.2 %copy-done = bf16[1024,2048]{1,0:T(8,128)(2,1)S(1)} copy-done((bf16[1024,2048]{1,0:T(8,128)(2,1)S(1)}, bf16[1024,2048]{1,0:T(8,128)(2,1)}, u32[]{:S(2)}) %copy-start) | copy-done | bytes 4194328
  81.9 1.6 project.1
  83.5 0.0 copy-start.1
  83.5 49.5 %all_to_all.20 = bf16[32,8,3072]{2,1,0:T(8,128)(2,1)S(1)} all-to-all(bf16[32,8,3072]{2,1,0:T(8,128)(2,1)S(1)} %bitcast.26), channel_id=1, replica_groups=mesh['ctx'=24,'exp'=32] {'exp'}, dimensions={0} | all-to-all | bytes 3145728 | tf_op jit(solution)/shard_map/all_to_all | solution.py:237
  133.1 0.0 copy-done.2
  133.1 0.0 copy-done.3
  133.1 0.0 copy-done.1
  133.1 3.2 %experts.1 = bf16[256,3072]{1,0:T(8,128)(2,1)S(1)} custom-call(bf16[256,3072]{1,0:T(8,128)(2,1)S(1)} %bitcast.21, bf16[2048,512]{1,0:T(8,128)(2,1)S(1)} %bitcast.23, bf16[2048,512]{1,0:T(8,128)(2,1)S(1)} %bitcast.24, bf16[512,2048]{1,0:T(8,128)(2,1)S(1)} %bitcast.25), custom_call_target="tpu_custom_call" | custom-call | tf_op jit(solution)/shard_map/experts/pallas_call | solution.py:186
  136.2 43.4 %all_to_all.21 = bf16[32,8,3072]{2,1,0:T(8,128)(2,1)S(1)} all-to-all(bf16[32,8,3072]{2,1,0:T(8,128)(2,1)S(1)} %bitcast.22), channel_id=1, replica_groups=mesh['ctx'=24,'exp'=32] {'exp'}, dimensions={0} | all-to-all | bytes 3145728 | tf_op jit(solution)/shard_map/all_to_all | solution.py:237
  179.7 1.9 %mix.1 = bf16[64,2048]{1,0:T(8,128)(2,1)} custom-call(bf16[256,3072]{1,0:T(8,128)(2,1)S(1)} %bitcast.20, f32[64,2048]{1,0:T(8,128)S(1)} %get-tuple-element.17.hidden_ref, bf16[3,256,64]{2,1,0:T(8,128)(2,1)S(1)} %get-tuple-element.18.m_ref, bf16[3,256,64]{2,1,0:T(8,128)(2,1)S(1)} %get-tuple-element.19.l_ref, bf16[3,256,64]{2,1,0:T(8,128)(2,1)S(1)} %get-tuple-element.20.h_ref), custom_call_target="tpu_custom_call" | custom-call | tf_op jit(solution)/shard_map/mix/pallas_call | solution.py:186
  (2 shorter events, 0.0 us)
Async XLA Ops:
  0.0 0.9 copy-start.5
  0.9 0.9 copy-start.6
  1.8 0.9 copy-start.7
  2.7 64.9 %copy-start.9 = (s32[1,64,4]{1,2,0:T(4,128)S(1)}, s32[1,64,4]{1,2,0:T(4,128)}, u32[]{:S(2)}) copy-start(s32[1,64,4]{1,2,0:T(4,128)} %param.20) | copy-start | bytes 3076
  2.7 64.9 %copy-start.10 = (f32[1,64,4]{1,2,0:T(4,128)S(1)}, f32[1,64,4]{1,2,0:T(4,128)}, u32[]{:S(2)}) copy-start(f32[1,64,4]{1,2,0:T(4,128)} %param.21) | copy-start | bytes 3076
  2.7 77.0 %copy-start.4 = (bf16[1,64,2048]{2,1,0:T(8,128)(2,1)S(1)}, bf16[1,64,2048]{2,1,0:T(8,128)(2,1)}, u32[]{:S(2)}) copy-start(bf16[1,64,2048]{2,1,0:T(8,128)(2,1)} %param.14) | copy-start | bytes 786436
  2.7 77.0 %copy-start.8 = (f32[2048]{0:T(1024)S(1)}, f32[2048]{0:T(1024)}, u32[]{:S(2)}) copy-start(f32[2048]{0:T(1024)} %param.16) | copy-start | bytes 24580
  3.8 53.5 %all-to-all-start = ((bf16[24,152,128]{2,1,0:T(8,128)(2,1)}), bf16[24,152,128]{2,1,0:T(8,128)(2,1)S(1)}, u32[]{:S(2)}, u32[]{:S(2)}) async-start(bf16[24,152,128]{2,1,0:T(8,128)(2,1)} %pack.1), calls=%async_computation | async-start | bytes 1867776 | tf_op jit(solution)/shard_map/all_to_all | solution.py:237
  59.6 20.0 %all-to-all-start.1 = ((bf16[24,24,128]{2,1,0:T(8,128)(2,1)}), bf16[24,24,128]{2,1,0:T(8,128)(2,1)S(1)}, u32[]{:S(2)}, u32[]{:S(2)}) async-start(bf16[24,24,128]{2,1,0:T(8,128)(2,1)} %attend.1), calls=%async_computation.1 | async-start | bytes 294912 | tf_op jit(solution)/shard_map/all_to_all | solution.py:237
  79.7 2.2 %copy-start = (bf16[1024,2048]{1,0:T(8,128)(2,1)S(1)}, bf16[1024,2048]{1,0:T(8,128)(2,1)}, u32[]{:S(2)}) copy-start(bf16[1024,2048]{1,0:T(8,128)(2,1)} %w_ref.1) | copy-start | bytes 12582916
  81.9 51.2 %copy-start.2 = (bf16[1,2048,512]{2,1,0:T(8,128)(2,1)S(1)}, bf16[1,2048,512]{2,1,0:T(8,128)(2,1)}, u32[]{:S(2)}) copy-start(bf16[1,2048,512]{2,1,0:T(8,128)(2,1)} %param.18) | copy-start | bytes 6291460
  81.9 51.2 %copy-start.3 = (bf16[1,512,2048]{2,1,0:T(8,128)(2,1)S(1)}, bf16[1,512,2048]{2,1,0:T(8,128)(2,1)}, u32[]{:S(2)}) copy-start(bf16[1,512,2048]{2,1,0:T(8,128)(2,1)} %param.19) | copy-start | bytes 6291460
  83.5 49.6 %copy-start.1 = (bf16[1,2048,512]{2,1,0:T(8,128)(2,1)S(1)}, bf16[1,2048,512]{2,1,0:T(8,128)(2,1)}, u32[]{:S(2)}) copy-start(bf16[1,2048,512]{2,1,0:T(8,128)(2,1)} %param.17) | copy-start | bytes 6291460

commit v3 on v2

v3 whole, which is shorter than its diff:
```python
import jax
import jax.numpy as jnp
from jax import lax
from jax.experimental import pallas as pl
from jax.experimental.pallas import tpu as pltpu
from jax.sharding import Mesh
from jax.sharding import PartitionSpec as P

HEADS = 8
HEAD_DIM = 128
TOP = 4
TOK = 64
D = 2048
FFW = 512
N_CTX = 24
EXPERTS = 32
PARTS = N_CTX // HEADS
Q_ROWS = 24
CHUNK = 2 * TOK + Q_ROWS
GROUP = 6
MAIN = 8
REST = 4
HALF = D // 2
WIDE = D + HALF
MODEL = HEADS * HEAD_DIM
HALF_MODEL = MODEL // 2
WIDE_MODEL = MODEL + HALF_MODEL
SLOT_ROWS = EXPERTS * MAIN
REST_ROWS = EXPERTS * REST
LANES = 128
RING = 8
QUAD = 4
f32 = jnp.float32
bf16 = jnp.bfloat16
i32 = jnp.int32


def dot(a, b):
    return jnp.dot(a, b, preferred_element_type=f32)


def dot_first(a, b):
    return lax.dot_general(a, b, (((0,), (0,)), ((), ())), preferred_element_type=f32)


def dot_last(a, b):
    return lax.dot_general(a, b, (((1,), (1,)), ((), ())), preferred_element_type=f32)


def part_rows(part):
    return min(Q_ROWS, TOK - part * Q_ROWS)


def pack_kernel(q_ref, k_ref, v_ref, o_ref):
    for head in range(HEADS):
        cols = slice(head * HEAD_DIM, (head + 1) * HEAD_DIM)
        for part in range(PARTS):
            rows = part_rows(part)
            chunk = head * PARTS + part
            o_ref[chunk, 0:TOK, :] = k_ref[:, cols]
            o_ref[chunk, TOK : 2 * TOK, :] = v_ref[:, cols]
            o_ref[chunk, 2 * TOK : 2 * TOK + rows, :] = q_ref[
                part * Q_ROWS : part * Q_ROWS + rows, cols
            ]
            if rows < Q_ROWS:
                o_ref[chunk, 2 * TOK + rows : CHUNK, :] = jnp.zeros((Q_ROWS - rows, HEAD_DIM), bf16)


def attend_kernel(part_ref, x_ref, o_ref):
    factor = HEAD_DIM ** (-0.5) * 1.4426950408889634
    rows = GROUP * Q_ROWS
    span = GROUP * TOK
    row = lax.broadcasted_iota(jnp.int32, (rows, span), 0)
    block = jnp.zeros((rows, span), jnp.int32)
    for b in range(1, GROUP):
        block = block + (row >= b * Q_ROWS).astype(jnp.int32)
    query_pos = row + block * (TOK - Q_ROWS) + part_ref[0] * Q_ROWS
    allowed = lax.broadcasted_iota(jnp.int32, (rows, span), 1) <= query_pos
    for g in range(N_CTX // GROUP):
        lo = g * GROUP
        hi = lo + GROUP
        queries = x_ref[lo:hi, 2 * TOK : CHUNK, :].reshape(rows, HEAD_DIM)
        near_keys = x_ref[lo:hi, 0:TOK, :].reshape(span, HEAD_DIM)
        near_values = x_ref[lo:hi, TOK : 2 * TOK, :].reshape(span, HEAD_DIM)
        near = jnp.where(allowed, dot_last(queries, near_keys), -1e30)
        top = jnp.max(near, axis=1, keepdims=True)
        if g:
            far_keys = x_ref[0:lo, 0:TOK, :].reshape(lo * TOK, HEAD_DIM)
            far_values = x_ref[0:lo, TOK : 2 * TOK, :].reshape(lo * TOK, HEAD_DIM)
            far = dot_last(queries, far_keys)
            top = jnp.maximum(top, jnp.max(far, axis=1, keepdims=True))
        near_exp = jnp.exp2((near - top) * factor)
        total = jnp.sum(near_exp, axis=1, keepdims=True)
        acc = dot(near_exp.astype(bf16), near_values)
        if g:
            far_exp = jnp.exp2((far - top) * factor)
            total = total + jnp.sum(far_exp, axis=1, keepdims=True)
            acc = acc + dot(far_exp.astype(bf16), far_values)
        o_ref[lo:hi] = (acc / total).astype(bf16).reshape(GROUP, Q_ROWS, HEAD_DIM)


def slots_of(routes):
    expert = lax.broadcasted_iota(i32, (EXPERTS, TOK), 0)
    named = jnp.zeros((EXPERTS, TOK), f32)
    for k in range(TOP):
        named = named + (routes[k : k + 1, :] == expert).astype(f32)
    earlier = (
        lax.broadcasted_iota(i32, (TOK, TOK), 0) < lax.broadcasted_iota(i32, (TOK, TOK), 1)
    ).astype(bf16)
    return named * (1.0 + dot(named.astype(bf16), earlier))


def masks_of(value):
    row = lax.broadcasted_iota(i32, value.shape, 0)
    main = value == ((row & 7) + 1).astype(f32)
    rest = value == ((row & 3) + 1 + MAIN).astype(f32)
    low = (row & 7) < REST
    return main, rest & low, rest & (~low)


def stage_kernel(residual_ref, routes_ref, o_ref):
    o_ref[:, 0:D] = residual_ref[...]
    row = lax.broadcasted_iota(i32, (TOK, EXPERTS), 0)
    expert = lax.broadcasted_iota(i32, (TOK, EXPERTS), 1)
    place = ((row >> 3) == (expert >> 2)) & ((row & 7) == (expert & 3))
    values = dot(place.astype(bf16), slots_of(routes_ref[...]).astype(bf16)).astype(bf16)
    o_ref[:, D : D + LANES] = jnp.concatenate([values, jnp.zeros((TOK, LANES - TOK), bf16)], axis=1)


def select_kernel(place_ref, *refs):
    row = lax.broadcasted_iota(i32, (TOK, TOK), 0)
    col = lax.broadcasted_iota(i32, (TOK, TOK), 1)
    y = (place_ref[0] + (row >> 3)) & (RING - 1)
    line = (col == y * 8 + place_ref[1]).astype(bf16)
    for source in range(QUAD):
        rows_ref = refs[source]
        value = dot(line, rows_ref[:, D : D + LANES])[:, 0:TOK]
        main, low, high = [mask.astype(bf16) for mask in masks_of(value)]
        whole = dot(main, rows_ref[:, 0:D]).astype(bf16)
        halves = (dot(low, rows_ref[:, 0:HALF]) + dot(high, rows_ref[:, HALF:D])).astype(bf16)
        for shift in range(RING):
            part = slice(shift * MAIN, (shift + 1) * MAIN)
            refs[QUAD + shift][source, :, 0:D] = whole[part]
            refs[QUAD + shift][source, :, D:WIDE] = halves[part]


def plan_kernel(routes_ref, prob_ref, *outs):
    routes = routes_ref[...]
    expert = lax.broadcasted_iota(i32, (EXPERTS, TOK), 0)
    prob = jnp.zeros((EXPERTS, TOK), f32)
    for k in range(TOP):
        prob = prob + jnp.where(routes[k : k + 1, :] == expert, prob_ref[k : k + 1, :], 0.0)
    spread = (
        (lax.broadcasted_iota(i32, (SLOT_ROWS, EXPERTS), 0) >> 3)
        == lax.broadcasted_iota(i32, (SLOT_ROWS, EXPERTS), 1)
    ).astype(bf16)
    masks = masks_of(dot(spread, slots_of(routes).astype(bf16)))
    for mask, out in zip(masks, outs[:3]):
        out[...] = mask.astype(bf16)
    for term in range(3):
        part = prob.astype(bf16)
        prob = prob - part.astype(f32)
        wide = dot(spread, part)
        for mask, out in zip(masks, outs[3:]):
            out[term] = jnp.where(mask, wide, 0.0).astype(bf16)


def dispatch_kernel(a_ref, m_ref, l_ref, h_ref, rows_ref, o_ref):
    for head in range(HEADS):
        cols = slice(head * HEAD_DIM, (head + 1) * HEAD_DIM)
        for part in range(PARTS):
            rows = part_rows(part)
            rows_ref[part * Q_ROWS : part * Q_ROWS + rows, cols] = a_ref[
                head * PARTS + part, 0:rows, :
            ]
    o_ref[:, 0:MODEL] = dot(m_ref[...], rows_ref[...]).astype(bf16)
    o_ref[:, MODEL:WIDE_MODEL] = (
        dot(l_ref[...], rows_ref[:, 0:HALF_MODEL]) + dot(h_ref[...], rows_ref[:, HALF_MODEL:MODEL])
    ).astype(bf16)


def hidden_kernel(rows_ref, residual_ref, w_ref, o_ref):
    o_ref[...] = residual_ref[...].astype(f32) + dot(rows_ref[...], w_ref[...])


def normed_of(residual, attended, w_ref, gain_ref):
    hidden = residual.astype(f32) + dot(attended, w_ref[...])
    mean_square = jnp.mean(hidden * hidden, axis=-1, keepdims=True)
    return (hidden * lax.rsqrt(mean_square + 1e-05) * gain_ref[...]).astype(bf16)


def picker(high):
    row = lax.broadcasted_iota(jnp.int32, (REST_ROWS, SLOT_ROWS), 0)
    col = lax.broadcasted_iota(jnp.int32, (REST_ROWS, SLOT_ROWS), 1)
    return (col == (row >> 2) * MAIN + (row & 3) + (REST if high else 0)).astype(bf16)


def expert_kernel(place_ref, x_ref, gain_ref, *refs):
    slots, weights = refs[:RING], refs[RING : RING + 4]
    o_ref, main_ref, rest_ref, rows_ref, w_ref, gate_ref, up_ref, down_ref, sems = refs[RING + 4 :]
    held = (w_ref, gate_ref, up_ref, down_ref)
    copies = [
        pltpu.make_async_copy(source, target, sems.at[i])
        for i, (source, target) in enumerate(zip(weights, held))
    ]
    for copy in copies:
        copy.start()
    for shift in range(RING):
        y = (place_ref[0] - shift) & (RING - 1)
        for source in range(QUAD):
            index = y * QUAD + (place_ref[1] ^ source)
            main_ref[index] = slots[shift][source, :, 0:D]
            rest_ref[index] = slots[shift][source, :, D:WIDE]
    low, high = picker(False), picker(True)
    copies[0].wait()
    rows_ref[0:SLOT_ROWS, :] = normed_of(
        main_ref[...].reshape(SLOT_ROWS, D), x_ref[:, 0:MODEL], w_ref, gain_ref
    )
    halves = rest_ref[...].reshape(SLOT_ROWS, HALF)
    residual = jnp.concatenate([dot(low, halves), dot(high, halves)], axis=1)
    halves = x_ref[:, MODEL:WIDE_MODEL]
    attended = jnp.concatenate([dot(low, halves), dot(high, halves)], axis=1).astype(bf16)
    rows_ref[SLOT_ROWS:, :] = normed_of(residual, attended, w_ref, gain_ref)
    copies[1].wait()
    gate = dot(rows_ref[...], gate_ref[...])
    copies[2].wait()
    up = dot(rows_ref[...], up_ref[...])
    copies[3].wait()
    act = (gate / (1.0 + jnp.exp(-gate)) * up).astype(bf16)
    made = dot(act, down_ref[...]).astype(bf16)
    o_ref[:, 0:D] = made[0:SLOT_ROWS]
    o_ref[:, D:WIDE] = (
        dot_first(low, made[SLOT_ROWS:, 0:HALF]) + dot_first(high, made[SLOT_ROWS:, HALF:D])
    ).astype(bf16)


def mix_kernel(y_ref, hidden_ref, m_ref, l_ref, h_ref, o_ref):
    total = hidden_ref[...]
    rest = y_ref[:, D:WIDE]
    first = jnp.zeros((TOK, HALF), f32)
    second = jnp.zeros((TOK, HALF), f32)
    for term in range(3):
        total = total + dot_first(m_ref[term], y_ref[:, 0:D])
        first = first + dot_first(l_ref[term], rest)
        second = second + dot_first(h_ref[term], rest)
    o_ref[:, 0:HALF] = (total[:, 0:HALF] + first).astype(bf16)
    o_ref[:, HALF:D] = (total[:, HALF:D] + second).astype(bf16)


def call(kernel, outs, *args, scratch=(), smem=0, away=0, mib=16):
    vmem = pl.BlockSpec(memory_space=pltpu.VMEM)
    specs = [pl.BlockSpec(memory_space=pltpu.SMEM)] * smem + [vmem] * (len(args) - smem - away)
    many = isinstance(outs, list)
    return pl.pallas_call(
        kernel,
        out_shape=outs,
        in_specs=specs + [pl.BlockSpec(memory_space=pltpu.HBM)] * away,
        out_specs=[vmem] * len(outs) if many else vmem,
        scratch_shapes=scratch,
        compiler_params=pltpu.CompilerParams(vmem_limit_bytes=mib * 1024 * 1024),
    )(*args)


def of(*dims, dtype=bf16):
    return jax.ShapeDtypeStruct(dims, dtype)


def pack(queries, keys, values):
    return call(pack_kernel, of(N_CTX, CHUNK, HEAD_DIM), queries, keys, values, mib=56)


def attend(part, gathered):
    return call(attend_kernel, of(N_CTX, Q_ROWS, HEAD_DIM), part, gathered, smem=1)


def plan(routes, prob):
    outs = [of(SLOT_ROWS, TOK)] * 3 + [of(3, SLOT_ROWS, TOK)] * 3
    made = call(plan_kernel, outs, routes.T, prob.T, mib=8)
    return made[:3], made[3:]


def stage(residual, routes):
    return call(stage_kernel, of(TOK, D + LANES), residual, routes.T, mib=8)


def select(place, rows):
    outs = [of(QUAD, MAIN, WIDE)] * RING
    return list(call(select_kernel, outs, place, *rows, smem=1, mib=16))


def dispatch(attended, masks):
    outs = [of(TOK, MODEL), of(SLOT_ROWS, WIDE_MODEL)]
    return call(dispatch_kernel, outs, attended, *masks, mib=8)


def hidden_of(rows, residual, out_proj):
    return call(hidden_kernel, of(TOK, D, dtype=f32), rows, residual, out_proj, mib=12)


def experts(place, rows, out_proj, norm_gain, weights, slots):
    scratch = [
        pltpu.VMEM((EXPERTS, MAIN, D), bf16),
        pltpu.VMEM((EXPERTS, MAIN, HALF), bf16),
        pltpu.VMEM((SLOT_ROWS + REST_ROWS, D), bf16),
        pltpu.VMEM((MODEL, D), bf16),
        pltpu.VMEM((D, FFW), bf16),
        pltpu.VMEM((D, FFW), bf16),
        pltpu.VMEM((FFW, D), bf16),
        pltpu.SemaphoreType.DMA((4,)),
    ]
    args = (rows, norm_gain.reshape(1, D), *slots, out_proj, *weights)
    outs = of(SLOT_ROWS, WIDE)
    return call(expert_kernel, outs, place, *args, scratch=scratch, smem=1, away=4, mib=50)


def mix(rows, hidden, probs):
    return call(mix_kernel, of(TOK, D), rows, hidden, *probs)


def exchange(x, axes):
    return lax.all_to_all(x, axes, split_axis=0, concat_axis=0, tiled=True)


def slots_exchange(x):
    return exchange(x.reshape(EXPERTS, MAIN, -1), ("y", "m")).reshape(SLOT_ROWS, -1)


def layer(
    queries, keys, values, residual, out_proj, norm_gain, w_gate, w_up, w_down, routes, route_prob
):
    part = (lax.axis_index("ctx") % PARTS).astype(i32).reshape(1)
    place = jnp.stack([lax.axis_index("y"), lax.axis_index("m")]).astype(i32)
    packed = pack(queries, keys, values)
    gathered = exchange(packed, "ctx")
    rows = [stage(residual, routes)]
    for other in range(1, QUAD):
        rows.append(lax.ppermute(rows[0], "m", [(i, i ^ other) for i in range(QUAD)]))
    slots = select(place, rows)
    for shift in range(1, RING):
        pairs = [(i, (i + shift) % RING) for i in range(RING)]
        slots[shift] = lax.ppermute(slots[shift], "y", pairs)
    masks, probs = plan(routes, route_prob)
    attended = attend(part, gathered)
    attended = exchange(attended, "ctx")
    rows, x = dispatch(attended, masks)
    x = slots_exchange(x)
    hidden = hidden_of(rows, residual, out_proj)
    x = experts(place, x, out_proj, norm_gain, (w_gate, w_up, w_down), slots)
    x = slots_exchange(x)
    return mix(x, hidden, probs)


def local(*args):
    args = [a if a.ndim < 3 else a[0] for a in args]
    return layer(*args)[None]


def solution(mesh):
    cut = Mesh(mesh.devices.reshape(N_CTX, RING, QUAD), ("ctx", "y", "m"))
    exp = ("y", "m")
    placed = (
        P(exp, "ctx", None),
        P(exp, "ctx", None),
        P(exp, "ctx", None),
        P(exp, "ctx", None),
        P(),
        P(),
        P(exp, None, None),
        P(exp, None, None),
        P(exp, None, None),
        P(exp, "ctx", None),
        P(exp, "ctx", None),
    )
    return jax.shard_map(
        local, mesh=cut, in_specs=placed, out_specs=P(exp, "ctx", None), check_vma=False
    )
```

time: 182 us -> 224 us (1.23)
  blocking collectives: 93 us -> 0 us
  waiting for transfers between devices: 46.7 us -> 121 us
  starting transfers between devices: 26.3 us -> 78.2 us
  Pallas kernels: 10.6 us -> 20.7 us
  local copies, waits for them, and re-layouts: 4.93 us -> 2.2 us
    all_to_all x2 -> x0, blocking collectives: 93 us -> none  [exchange(): return lax.all_to_all(x, axis, split_axis=0, concat_axis=0, tiled=True)]
    ppermute x0 -> x10, waiting for transfers between devices: none -> 38.6 us  [the longest x7 23 us: layer(): slots[shift] = lax.ppermute(slots[shift], 'y', pairs)]
    all_to_all x2 -> x4, waiting for transfers between devices: 46.7 us -> 82.8 us  [exchange(): return lax.all_to_all(x, axes, split_axis=0, concat_axis=0, tiled=True)]
    ppermute x0 -> x10, starting transfers between devices: none -> 35.5 us  [the longest x7 27.6 us: layer(): slots[shift] = lax.ppermute(slots[shift], 'y', pairs)]
    all_to_all x2 -> x4, starting transfers between devices: 26.3 us -> 42.7 us  [exchange(): return lax.all_to_all(x, axes, split_axis=0, concat_axis=0, tiled=True)]
    pallas_call x6 -> x9, Pallas kernels: 10.6 us -> 20.7 us  [call(): pl.pallas_call(kernel, out_shape=outs, in_specs=specs + [pl.BlockSpec(mem...]
    unnamed x22 -> x10, local copies, waits for them, and re-layouts: 4.93 us -> 2.2 us
  transfers between devices with their start and end apart: 2 -> 14, of which waited for: 2 -> 9; matrix products, arithmetic and copies ran while one was open for 0% -> 0% of each run, Pallas kernels for 0% -> 1%
where the time goes in v3:
time: 224 us; the launch traced here: 223 us
  waiting for transfers between devices  121 us (54%)
  starting transfers between devices  78.2 us (35%)
  Pallas kernels  20.7 us (9%)
    all_to_all x4, waiting for transfers between devices, exchange(): return lax.all_to_all(x, axes, split_axis=0, concat_axis=0, tiled=True)  82.8 us
    all_to_all x4, starting transfers between devices, exchange(): return lax.all_to_all(x, axes, split_axis=0, concat_axis=0, tiled=True)  42.7 us
    ppermute x7, starting transfers between devices, layer(): slots[shift] = lax.ppermute(slots[shift], 'y', pairs)  27.6 us
    ppermute x7, waiting for transfers between devices, layer(): slots[shift] = lax.ppermute(slots[shift], 'y', pairs)  23 us
    pallas_call x9, Pallas kernels, call(): pl.pallas_call(kernel, out_shape=outs, in_specs=specs + [pl.BlockSpec(mem...  20.7 us
    ppermute x3, waiting for transfers between devices, layer(): lax.ppermute(rows[0], 'm', [(i, i ^ other) for i in range(QUAD)])  15.6 us
    ppermute x3, starting transfers between devices, layer(): lax.ppermute(rows[0], 'm', [(i, i ^ other) for i in range(QUAD)])  7.86 us
  transfers between devices with their start and end apart: 14, of which 9 were waited for; matrix products, arithmetic and copies ran while one was open for 0% of the time, Pallas kernels for 1%

profile of v3, /device:TPU:1, one launch (start us, length us, event | category | flops | bytes accessed | tf_op | source)
XLA Modules:
  0.0 222.9 jit_solution(15983725059554247459)
XLA Ops:
  0.0 2.1 shard_map.109
  2.1 18.4 %all-to-all-start = ((bf16[24,152,128]{2,1,0:T(8,128)(2,1)}), bf16[24,152,128]{2,1,0:T(8,128)(2,1)S(1)}, u32[]{:S(2)}, u32[]{:S(2)}) async-start(bf16[24,152,128]{2,1,0:T(8,128)(2,1)} %shard_map.109), calls=%async_computation | async-start | bytes 1867776 | tf_op jit(solution)/shard_map/all_to_all | solution.py:321
  20.5 35.1 %all-to-all-done.x_ref = bf16[24,152,128]{2,1,0:T(8,128)(2,1)S(1)} async-done(((bf16[24,152,128]{2,1,0:T(8,128)(2,1)}), bf16[24,152,128]{2,1,0:T(8,128)(2,1)S(1)}, u32[]{:S(2)}, u32[]{:S(2)}) %all-to-all-start) | async-done | bytes 933920 | tf_op jit(solution)/shard_map/all_to_all | solution.py:321
  55.6 2.4 %shard_map.110 = bf16[24,24,128]{2,1,0:T(8,128)(2,1)} custom-call(s32[1]{0:T(128)} %bitcast.2.part_ref, bf16[24,152,128]{2,1,0:T(8,128)(2,1)S(1)} %all-to-all-done.x_ref), custom_call_target="tpu_custom_call" | custom-call | tf_op jit(solution)/shard_map/pallas_call | solution.py:254
  58.0 8.1 %all-to-all-start.1 = ((bf16[24,24,128]{2,1,0:T(8,128)(2,1)}), bf16[24,24,128]{2,1,0:T(8,128)(2,1)S(1)}, u32[]{:S(2)}, u32[]{:S(2)}) async-start(bf16[24,24,128]{2,1,0:T(8,128)(2,1)} %shard_map.110), calls=%async_computation.1 | async-start | bytes 294912 | tf_op jit(solution)/shard_map/all_to_all | solution.py:321
  66.1 0.4 shard_map.111
  66.6 11.6 %all-to-all-done.1.a_ref = bf16[24,24,128]{2,1,0:T(8,128)(2,1)S(1)} async-done(((bf16[24,24,128]{2,1,0:T(8,128)(2,1)}), bf16[24,24,128]{2,1,0:T(8,128)(2,1)S(1)}, u32[]{:S(2)}, u32[]{:S(2)}) %all-to-all-start.1) | async-done | bytes 147488 | tf_op jit(solution)/shard_map/all_to_all | solution.py:321
  78.2 1.3 shard_map.112
  79.5 10.4 %all-to-all-start.2 = ((bf16[32,8,1536]{2,1,0:T(8,128)(2,1)}), bf16[32,8,1536]{2,1,0:T(8,128)(2,1)S(1)}, u32[]{:S(2)}, u32[]{:S(2)}) async-start(bf16[32,8,1536]{2,1,0:T(8,128)(2,1)} %bitcast.10), calls=%async_computation.2 | async-start | bytes 1572864 | tf_op jit(solution)/shard_map/all_to_all | solution.py:321
  90.1 3.5 %collective-permute-start.2 = (bf16[64,2176]{1,0:T(8,128)(2,1)S(1)}, bf16[64,2176]{1,0:T(8,128)(2,1)S(1)}, u32[]{:S(2)}, u32[]{:S(2)}) collective-permute-start(bf16[64,2176]{1,0:T(8,128)(2,1)S(1)} %shard_map.113.refs_0_), channel_id=1, source_target_pairs={{0,3},{1,2},{2,1},{3,0},{4,7},{5,6},{6,5},{7,4},{8,11},{9,10},{10,... | collective-permute-start | bytes 835592 | tf_op jit(solution)/shard_map/ppermute | solution.py:337
  93.7 1.9 collective-permute-start.1
  95.6 2.4 %collective-permute-start = (bf16[64,2176]{1,0:T(8,128)(2,1)S(1)}, bf16[64,2176]{1,0:T(8,128)(2,1)S(1)}, u32[]{:S(2)}, u32[]{:S(2)}) collective-permute-start(bf16[64,2176]{1,0:T(8,128)(2,1)S(1)} %shard_map.113.refs_0_), channel_id=1, source_target_pairs={{0,1},{1,0},{2,3},{3,2},{4,5},{5,4},{6,7},{7,6},{8,9},{9,8},{10,11... | collective-permute-start | bytes 835592 | tf_op jit(solution)/shard_map/ppermute | solution.py:337
  98.1 9.2 %collective-permute-done.2.refs_3_ = bf16[64,2176]{1,0:T(8,128)(2,1)S(1)} collective-permute-done((bf16[64,2176]{1,0:T(8,128)(2,1)S(1)}, bf16[64,2176]{1,0:T(8,128)(2,1)S(1)}, u32[]{:S(2)}, u32[]{:S(2)}) %collective-permute-start.2) | collective-permute-done | bytes 278560 | tf_op jit(solution)/shard_map/ppermute | solution.py:337
  107.3 6.4 %collective-permute-done.1.refs_2_ = bf16[64,2176]{1,0:T(8,128)(2,1)S(1)} collective-permute-done((bf16[64,2176]{1,0:T(8,128)(2,1)S(1)}, bf16[64,2176]{1,0:T(8,128)(2,1)S(1)}, u32[]{:S(2)}, u32[]{:S(2)}) %collective-permute-start.1) | collective-permute-done | bytes 278560 | tf_op jit(solution)/shard_map/ppermute | solution.py:337
  113.7 1.8 shard_map.114
  115.5 3.5 %collective-permute-start.3 = (bf16[4,8,3072]{2,1,0:T(8,128)(2,1)S(1)}, bf16[4,8,3072]{2,1,0:T(8,128)(2,1)S(1)}, u32[]{:S(2)}, u32[]{:S(2)}) collective-permute-start(bf16[4,8,3072]{2,1,0:T(8,128)(2,1)S(1)} %get-tuple-element.26), channel_id=1, source_target_pairs={{0,4},{4,8},{8,12},{12,16},{16,20},{20,24},{24,28},{28,0},{1,5},{5... | collective-permute-start | bytes 589832 | tf_op jit(solution)/shard_map/ppermute | solution.py:341
  119.0 3.6 %collective-permute-start.4 = (bf16[4,8,3072]{2,1,0:T(8,128)(2,1)S(1)}, bf16[4,8,3072]{2,1,0:T(8,128)(2,1)S(1)}, u32[]{:S(2)}, u32[]{:S(2)}) collective-permute-start(bf16[4,8,3072]{2,1,0:T(8,128)(2,1)S(1)} %get-tuple-element.27), channel_id=1, source_target_pairs={{0,8},{4,12},{8,16},{12,20},{16,24},{20,28},{24,0},{28,4},{1,9},{5... | collective-permute-start | bytes 589832 | tf_op jit(solution)/shard_map/ppermute | solution.py:341
  122.6 4.2 %collective-permute-start.5 = (bf16[4,8,3072]{2,1,0:T(8,128)(2,1)S(1)}, bf16[4,8,3072]{2,1,0:T(8,128)(2,1)S(1)}, u32[]{:S(2)}, u32[]{:S(2)}) collective-permute-start(bf16[4,8,3072]{2,1,0:T(8,128)(2,1)S(1)} %get-tuple-element.28), channel_id=1, source_target_pairs={{0,12},{4,16},{8,20},{12,24},{16,28},{20,0},{24,4},{28,8},{1,13},{... | collective-permute-start | bytes 589832 | tf_op jit(solution)/shard_map/ppermute | solution.py:341
  126.9 4.0 %collective-permute-start.6 = (bf16[4,8,3072]{2,1,0:T(8,128)(2,1)S(1)}, bf16[4,8,3072]{2,1,0:T(8,128)(2,1)S(1)}, u32[]{:S(2)}, u32[]{:S(2)}) collective-permute-start(bf16[4,8,3072]{2,1,0:T(8,128)(2,1)S(1)} %get-tuple-element.29), channel_id=1, source_target_pairs={{0,16},{4,20},{8,24},{12,28},{16,0},{20,4},{24,8},{28,12},{1,17},{... | collective-permute-start | bytes 589832 | tf_op jit(solution)/shard_map/ppermute | solution.py:341
  130.8 4.4 %collective-permute-start.7 = (bf16[4,8,3072]{2,1,0:T(8,128)(2,1)S(1)}, bf16[4,8,3072]{2,1,0:T(8,128)(2,1)S(1)}, u32[]{:S(2)}, u32[]{:S(2)}) collective-permute-start(bf16[4,8,3072]{2,1,0:T(8,128)(2,1)S(1)} %get-tuple-element.30), channel_id=1, source_target_pairs={{0,20},{4,24},{8,28},{12,0},{16,4},{20,8},{24,12},{28,16},{1,21},{... | collective-permute-start | bytes 589832 | tf_op jit(solution)/shard_map/ppermute | solution.py:341
  135.3 5.2 %collective-permute-start.8 = (bf16[4,8,3072]{2,1,0:T(8,128)(2,1)S(1)}, bf16[4,8,3072]{2,1,0:T(8,128)(2,1)S(1)}, u32[]{:S(2)}, u32[]{:S(2)}) collective-permute-start(bf16[4,8,3072]{2,1,0:T(8,128)(2,1)S(1)} %get-tuple-element.31), channel_id=1, source_target_pairs={{0,24},{4,28},{8,0},{12,4},{16,8},{20,12},{24,16},{28,20},{1,25},{... | collective-permute-start | bytes 589832 | tf_op jit(solution)/shard_map/ppermute | solution.py:341
  140.5 2.7 %collective-permute-start.9 = (bf16[4,8,3072]{2,1,0:T(8,128)(2,1)S(1)}, bf16[4,8,3072]{2,1,0:T(8,128)(2,1)S(1)}, u32[]{:S(2)}, u32[]{:S(2)}) collective-permute-start(bf16[4,8,3072]{2,1,0:T(8,128)(2,1)S(1)} %get-tuple-element.32), channel_id=1, source_target_pairs={{0,28},{4,0},{8,4},{12,8},{16,12},{20,16},{24,20},{28,24},{1,29},{... | collective-permute-start | bytes 589832 | tf_op jit(solution)/shard_map/ppermute | solution.py:341
  143.2 9.2 %collective-permute-done.6.refs_4_ = bf16[4,8,3072]{2,1,0:T(8,128)(2,1)S(1)} collective-permute-done((bf16[4,8,3072]{2,1,0:T(8,128)(2,1)S(1)}, bf16[4,8,3072]{2,1,0:T(8,128)(2,1)S(1)}, u32[]{:S(2)}, u32[]{:S(2)}) %collective-permute-start.6) | collective-permute-done | bytes 196640 | tf_op jit(solution)/shard_map/ppermute | solution.py:341
  152.4 1.8 collective-permute-done.7.refs_5_
  154.2 10.5 %collective-permute-done.8.refs_6_ = bf16[4,8,3072]{2,1,0:T(8,128)(2,1)S(1)} collective-permute-done((bf16[4,8,3072]{2,1,0:T(8,128)(2,1)S(1)}, bf16[4,8,3072]{2,1,0:T(8,128)(2,1)S(1)}, u32[]{:S(2)}, u32[]{:S(2)}) %collective-permute-start.8) | collective-permute-done | bytes 196640 | tf_op jit(solution)/shard_map/ppermute | solution.py:341
  164.7 1.5 collective-permute-done.9.refs_7_
  166.2 9.6 %shard_map.115 = bf16[256,3072]{1,0:T(8,128)(2,1)} custom-call(s32[2]{0:T(128)S(1)} %pad_add_fusion.place_ref, bf16[256,1536]{1,0:T(8,128)(2,1)S(1)} %bitcast.23, f32[1,2048]{1,0:T(1,128)S(1)} %bitcast.26, bf16[4,8,3072]{2,1,0:T(8,128)(2,1)S(1)} %get-tuple-element.25.refs_0_, bf16[4,8,3072]{2,1,0:T(8,128)(2,1)S(1)} %collective-permute-done.3.refs_1_, ...), custom_call_target="tpu_custom_call" | custom-call | tf_op jit(solution)/shard_map/pallas_call | solution.py:254
  175.8 5.9 %all-to-all-start.3 = ((bf16[32,8,3072]{2,1,0:T(8,128)(2,1)}), bf16[32,8,3072]{2,1,0:T(8,128)(2,1)S(1)}, u32[]{:S(2)}, u32[]{:S(2)}) async-start(bf16[32,8,3072]{2,1,0:T(8,128)(2,1)} %bitcast.18), calls=%async_computation.3 | async-start | bytes 3145728 | tf_op jit(solution)/shard_map/all_to_all | solution.py:321
  181.8 2.2 copy-done
  183.9 0.8 shard_map.116.hidden_ref
  184.8 36.1 %all-to-all-done.3 = bf16[32,8,3072]{2,1,0:T(8,128)(2,1)S(1)} async-done(((bf16[32,8,3072]{2,1,0:T(8,128)(2,1)}), bf16[32,8,3072]{2,1,0:T(8,128)(2,1)S(1)}, u32[]{:S(2)}, u32[]{:S(2)}) %all-to-all-start.3) | async-done | bytes 1572896 | tf_op jit(solution)/shard_map/all_to_all | solution.py:321
  220.9 1.9 shard_map.117
  (16 shorter events, 0.4 us)
Async XLA Ops:
  0.0 66.1 %copy-start.3 = (s32[1,64,4]{1,2,0:T(4,128)S(1)}, s32[1,64,4]{1,2,0:T(4,128)}, u32[]{:S(2)}) copy-start(s32[1,64,4]{1,2,0:T(4,128)} %param.20) | copy-start | bytes 3076
  0.0 66.1 %copy-start.4 = (f32[1,64,4]{1,2,0:T(4,128)S(1)}, f32[1,64,4]{1,2,0:T(4,128)}, u32[]{:S(2)}) copy-start(f32[1,64,4]{1,2,0:T(4,128)} %param.21) | copy-start | bytes 3076
  2.1 53.5 %all-to-all-start = ((bf16[24,152,128]{2,1,0:T(8,128)(2,1)}), bf16[24,152,128]{2,1,0:T(8,128)(2,1)S(1)}, u32[]{:S(2)}, u32[]{:S(2)}) async-start(bf16[24,152,128]{2,1,0:T(8,128)(2,1)} %shard_map.109), calls=%async_computation | async-start | bytes 1867776 | tf_op jit(solution)/shard_map/all_to_all | solution.py:321
  20.5 69.4 %copy-start.1 = (bf16[1,64,2048]{2,1,0:T(8,128)(2,1)S(1)}, bf16[1,64,2048]{2,1,0:T(8,128)(2,1)}, u32[]{:S(2)}) copy-start(bf16[1,64,2048]{2,1,0:T(8,128)(2,1)} %param.14) | copy-start | bytes 786436
  58.0 108.2 %copy-start.2 = (f32[2048]{0:T(1024)S(1)}, f32[2048]{0:T(1024)}, u32[]{:S(2)}) copy-start(f32[2048]{0:T(1024)} %param.16) | copy-start | bytes 24580
  58.0 20.2 %all-to-all-start.1 = ((bf16[24,24,128]{2,1,0:T(8,128)(2,1)}), bf16[24,24,128]{2,1,0:T(8,128)(2,1)S(1)}, u32[]{:S(2)}, u32[]{:S(2)}) async-start(bf16[24,24,128]{2,1,0:T(8,128)(2,1)} %shard_map.110), calls=%async_computation.1 | async-start | bytes 294912 | tf_op jit(solution)/shard_map/all_to_all | solution.py:321
  79.5 86.7 %all-to-all-start.2 = ((bf16[32,8,1536]{2,1,0:T(8,128)(2,1)}), bf16[32,8,1536]{2,1,0:T(8,128)(2,1)S(1)}, u32[]{:S(2)}, u32[]{:S(2)}) async-start(bf16[32,8,1536]{2,1,0:T(8,128)(2,1)} %bitcast.10), calls=%async_computation.2 | async-start | bytes 1572864 | tf_op jit(solution)/shard_map/all_to_all | solution.py:321
  90.1 17.2 %collective-permute-start.2 = (bf16[64,2176]{1,0:T(8,128)(2,1)S(1)}, bf16[64,2176]{1,0:T(8,128)(2,1)S(1)}, u32[]{:S(2)}, u32[]{:S(2)}) collective-permute-start(bf16[64,2176]{1,0:T(8,128)(2,1)S(1)} %shard_map.113.refs_0_), channel_id=1, source_target_pairs={{0,3},{1,2},{2,1},{3,0},{4,7},{5,6},{6,5},{7,4},{8,11},{9,10},{10,... | collective-permute-start | bytes 835592 | tf_op jit(solution)/shard_map/ppermute | solution.py:337
  93.7 20.0 %collective-permute-start.1 = (bf16[64,2176]{1,0:T(8,128)(2,1)S(1)}, bf16[64,2176]{1,0:T(8,128)(2,1)S(1)}, u32[]{:S(2)}, u32[]{:S(2)}) collective-permute-start(bf16[64,2176]{1,0:T(8,128)(2,1)S(1)} %shard_map.113.refs_0_), channel_id=1, source_target_pairs={{0,2},{1,3},{2,0},{3,1},{4,6},{5,7},{6,4},{7,5},{8,10},{9,11},{10,... | collective-permute-start | bytes 835592 | tf_op jit(solution)/shard_map/ppermute | solution.py:337
  95.6 18.1 %collective-permute-start = (bf16[64,2176]{1,0:T(8,128)(2,1)S(1)}, bf16[64,2176]{1,0:T(8,128)(2,1)S(1)}, u32[]{:S(2)}, u32[]{:S(2)}) collective-permute-start(bf16[64,2176]{1,0:T(8,128)(2,1)S(1)} %shard_map.113.refs_0_), channel_id=1, source_target_pairs={{0,1},{1,0},{2,3},{3,2},{4,5},{5,4},{6,7},{7,6},{8,9},{9,8},{10,11... | collective-permute-start | bytes 835592 | tf_op jit(solution)/shard_map/ppermute | solution.py:337
  115.5 19.7 %collective-permute-start.3 = (bf16[4,8,3072]{2,1,0:T(8,128)(2,1)S(1)}, bf16[4,8,3072]{2,1,0:T(8,128)(2,1)S(1)}, u32[]{:S(2)}, u32[]{:S(2)}) collective-permute-start(bf16[4,8,3072]{2,1,0:T(8,128)(2,1)S(1)} %get-tuple-element.26), channel_id=1, source_target_pairs={{0,4},{4,8},{8,12},{12,16},{16,20},{20,24},{24,28},{28,0},{1,5},{5... | collective-permute-start | bytes 589832 | tf_op jit(solution)/shard_map/ppermute | solution.py:341
  119.0 21.5 %collective-permute-start.4 = (bf16[4,8,3072]{2,1,0:T(8,128)(2,1)S(1)}, bf16[4,8,3072]{2,1,0:T(8,128)(2,1)S(1)}, u32[]{:S(2)}, u32[]{:S(2)}) collective-permute-start(bf16[4,8,3072]{2,1,0:T(8,128)(2,1)S(1)} %get-tuple-element.27), channel_id=1, source_target_pairs={{0,8},{4,12},{8,16},{12,20},{16,24},{20,28},{24,0},{28,4},{1,9},{5... | collective-permute-start | bytes 589832 | tf_op jit(solution)/shard_map/ppermute | solution.py:341
  122.6 20.6 %collective-permute-start.5 = (bf16[4,8,3072]{2,1,0:T(8,128)(2,1)S(1)}, bf16[4,8,3072]{2,1,0:T(8,128)(2,1)S(1)}, u32[]{:S(2)}, u32[]{:S(2)}) collective-permute-start(bf16[4,8,3072]{2,1,0:T(8,128)(2,1)S(1)} %get-tuple-element.28), channel_id=1, source_target_pairs={{0,12},{4,16},{8,20},{12,24},{16,28},{20,0},{24,4},{28,8},{1,13},{... | collective-permute-start | bytes 589832 | tf_op jit(solution)/shard_map/ppermute | solution.py:341
  126.9 25.6 %collective-permute-start.6 = (bf16[4,8,3072]{2,1,0:T(8,128)(2,1)S(1)}, bf16[4,8,3072]{2,1,0:T(8,128)(2,1)S(1)}, u32[]{:S(2)}, u32[]{:S(2)}) collective-permute-start(bf16[4,8,3072]{2,1,0:T(8,128)(2,1)S(1)} %get-tuple-element.29), channel_id=1, source_target_pairs={{0,16},{4,20},{8,24},{12,28},{16,0},{20,4},{24,8},{28,12},{1,17},{... | collective-permute-start | bytes 589832 | tf_op jit(solution)/shard_map/ppermute | solution.py:341
  130.8 23.4 %collective-permute-start.7 = (bf16[4,8,3072]{2,1,0:T(8,128)(2,1)S(1)}, bf16[4,8,3072]{2,1,0:T(8,128)(2,1)S(1)}, u32[]{:S(2)}, u32[]{:S(2)}) collective-permute-start(bf16[4,8,3072]{2,1,0:T(8,128)(2,1)S(1)} %get-tuple-element.30), channel_id=1, source_target_pairs={{0,20},{4,24},{8,28},{12,0},{16,4},{20,8},{24,12},{28,16},{1,21},{... | collective-permute-start | bytes 589832 | tf_op jit(solution)/shard_map/ppermute | solution.py:341
  135.3 29.4 %collective-permute-start.8 = (bf16[4,8,3072]{2,1,0:T(8,128)(2,1)S(1)}, bf16[4,8,3072]{2,1,0:T(8,128)(2,1)S(1)}, u32[]{:S(2)}, u32[]{:S(2)}) collective-permute-start(bf16[4,8,3072]{2,1,0:T(8,128)(2,1)S(1)} %get-tuple-element.31), channel_id=1, source_target_pairs={{0,24},{4,28},{8,0},{12,4},{16,8},{20,12},{24,16},{28,20},{1,25},{... | collective-permute-start | bytes 589832 | tf_op jit(solution)/shard_map/ppermute | solution.py:341
  140.5 25.7 %collective-permute-start.9 = (bf16[4,8,3072]{2,1,0:T(8,128)(2,1)S(1)}, bf16[4,8,3072]{2,1,0:T(8,128)(2,1)S(1)}, u32[]{:S(2)}, u32[]{:S(2)}) collective-permute-start(bf16[4,8,3072]{2,1,0:T(8,128)(2,1)S(1)} %get-tuple-element.32), channel_id=1, source_target_pairs={{0,28},{4,0},{8,4},{12,8},{16,12},{20,16},{24,20},{28,24},{1,29},{... | collective-permute-start | bytes 589832 | tf_op jit(solution)/shard_map/ppermute | solution.py:341
  175.8 45.1 %all-to-all-start.3 = ((bf16[32,8,3072]{2,1,0:T(8,128)(2,1)}), bf16[32,8,3072]{2,1,0:T(8,128)(2,1)S(1)}, u32[]{:S(2)}, u32[]{:S(2)}) async-start(bf16[32,8,3072]{2,1,0:T(8,128)(2,1)} %bitcast.18), calls=%async_computation.3 | async-start | bytes 3145728 | tf_op jit(solution)/shard_map/all_to_all | solution.py:321
  181.7 2.2 copy-start

commit v4 on v3

--- a/solution.py
+++ b/solution.py
@@ -30,6 +30,8 @@
 LANES = 128
 RING = 8
 QUAD = 4
+FAR = 4
+CODES = (0, 2, 1, 3)
 f32 = jnp.float32
 bf16 = jnp.bfloat16
 i32 = jnp.int32
@@ -128,20 +130,53 @@
 
 
 def select_kernel(place_ref, *refs):
-    row = lax.broadcasted_iota(i32, (TOK, TOK), 0)
+    m = place_ref[1]
+    step = 2 * (m & 1) - 1
+    row = lax.broadcasted_iota(i32, (TOK, TOK), 0) >> 3
     col = lax.broadcasted_iota(i32, (TOK, TOK), 1)
-    y = (place_ref[0] + (row >> 3)) & (RING - 1)
-    line = (col == y * 8 + place_ref[1]).astype(bf16)
-    for source in range(QUAD):
-        rows_ref = refs[source]
+    other = row > FAR
+    y = (place_ref[0] + step * jnp.where(other, row - FAR, row)) & (RING - 1)
+    line = (col == y * 8 + jnp.where(other, m ^ 1, m)).astype(bf16)
+    own_ref, far_ref, *pair_refs = refs[3:]
+    mine_ref, beside_ref, others_ref = refs[:3]
+    for source, rows_ref in enumerate((mine_ref, beside_ref, others_ref.at[0], others_ref.at[1])):
         value = dot(line, rows_ref[:, D : D + LANES])[:, 0:TOK]
         main, low, high = [mask.astype(bf16) for mask in masks_of(value)]
         whole = dot(main, rows_ref[:, 0:D]).astype(bf16)
         halves = (dot(low, rows_ref[:, 0:HALF]) + dot(high, rows_ref[:, HALF:D])).astype(bf16)
-        for shift in range(RING):
-            part = slice(shift * MAIN, (shift + 1) * MAIN)
-            refs[QUAD + shift][source, :, 0:D] = whole[part]
-            refs[QUAD + shift][source, :, D:WIDE] = halves[part]
+        for index in range(2 * FAR):
+            part = slice(index * MAIN, (index + 1) * MAIN)
+            if index == 0:
+                out = own_ref.at[source]
+            elif index == FAR:
+                out = far_ref.at[source]
+            else:
+                out = pair_refs[index % FAR - 1].at[index // FAR, source]
+            out[:, 0:D] = whole[part]
+            out[:, D:WIDE] = halves[part]
+
+
+def order_kernel(place_ref, own_ref, far_ref, *refs):
+    pair_refs, (mate_ref, o_ref, main_ref, rest_ref) = refs[: FAR - 1], refs[FAR - 1 :]
+    y, m = place_ref[0], place_ref[1]
+    step = 2 * (m & 1) - 1
+
+    def put(ref, index, away, flip):
+        row = (y + away) & (RING - 1)
+        for source in range(QUAD):
+            target = row * QUAD + (m ^ flip ^ CODES[source])
+            main_ref[target] = ref[(*index, source)][:, 0:D]
+            rest_ref[target] = ref[(*index, source)][:, D:WIDE]
+
+    put(own_ref, (), 0, 0)
+    put(far_ref, (), FAR, 0)
+    for j in range(1, FAR):
+        put(pair_refs[j - 1], (0,), -step * j, 0)
+        put(mate_ref, (j - 1,), step * j, 1)
+    o_ref[0:SLOT_ROWS, :] = main_ref[...].reshape(SLOT_ROWS, D)
+    halves = rest_ref[...].reshape(SLOT_ROWS, HALF)
+    o_ref[SLOT_ROWS:, 0:HALF] = dot(picker(False), halves).astype(bf16)
+    o_ref[SLOT_ROWS:, HALF:D] = dot(picker(True), halves).astype(bf16)
 
 
 def plan_kernel(routes_ref, prob_ref, *outs):
@@ -195,42 +230,32 @@
     return (col == (row >> 2) * MAIN + (row & 3) + (REST if high else 0)).astype(bf16)
 
 
-def expert_kernel(place_ref, x_ref, gain_ref, *refs):
-    slots, weights = refs[:RING], refs[RING : RING + 4]
-    o_ref, main_ref, rest_ref, rows_ref, w_ref, gate_ref, up_ref, down_ref, sems = refs[RING + 4 :]
-    held = (w_ref, gate_ref, up_ref, down_ref)
+def expert_kernel(x_ref, residual_ref, w_ref, gain_ref, *refs):
+    weights, (o_ref, rows_ref, *held, sems) = refs[:3], refs[3:]
+    gate_ref, up_ref, down_ref = held
     copies = [
         pltpu.make_async_copy(source, target, sems.at[i])
         for i, (source, target) in enumerate(zip(weights, held))
     ]
     for copy in copies:
         copy.start()
-    for shift in range(RING):
-        y = (place_ref[0] - shift) & (RING - 1)
-        for source in range(QUAD):
-            index = y * QUAD + (place_ref[1] ^ source)
-            main_ref[index] = slots[shift][source, :, 0:D]
-            rest_ref[index] = slots[shift][source, :, D:WIDE]
     low, high = picker(False), picker(True)
-    copies[0].wait()
-    rows_ref[0:SLOT_ROWS, :] = normed_of(
-        main_ref[...].reshape(SLOT_ROWS, D), x_ref[:, 0:MODEL], w_ref, gain_ref
-    )
-    halves = rest_ref[...].reshape(SLOT_ROWS, HALF)
-    residual = jnp.concatenate([dot(low, halves), dot(high, halves)], axis=1)
+    main = slice(0, SLOT_ROWS)
+    rest = slice(SLOT_ROWS, SLOT_ROWS + REST_ROWS)
+    rows_ref[main, :] = normed_of(residual_ref[main, :], x_ref[:, 0:MODEL], w_ref, gain_ref)
     halves = x_ref[:, MODEL:WIDE_MODEL]
     attended = jnp.concatenate([dot(low, halves), dot(high, halves)], axis=1).astype(bf16)
-    rows_ref[SLOT_ROWS:, :] = normed_of(residual, attended, w_ref, gain_ref)
+    rows_ref[rest, :] = normed_of(residual_ref[rest, :], attended, w_ref, gain_ref)
+    copies[0].wait()
+    gate = dot(rows_ref[...], gate_ref[...])
     copies[1].wait()
-    gate = dot(rows_ref[...], gate_ref[...])
+    up = dot(rows_ref[...], up_ref[...])
+    act = (gate / (1.0 + jnp.exp(-gate)) * up).astype(bf16)
     copies[2].wait()
-    up = dot(rows_ref[...], up_ref[...])
-    copies[3].wait()
-    act = (gate / (1.0 + jnp.exp(-gate)) * up).astype(bf16)
     made = dot(act, down_ref[...]).astype(bf16)
-    o_ref[:, 0:D] = made[0:SLOT_ROWS]
+    o_ref[:, 0:D] = made[main]
     o_ref[:, D:WIDE] = (
-        dot_first(low, made[SLOT_ROWS:, 0:HALF]) + dot_first(high, made[SLOT_ROWS:, HALF:D])
+        dot_first(low, made[rest, 0:HALF]) + dot_first(high, made[rest, HALF:D])
     ).astype(bf16)
 
 
@@ -284,8 +309,16 @@
 
 
 def select(place, rows):
-    outs = [of(QUAD, MAIN, WIDE)] * RING
-    return list(call(select_kernel, outs, place, *rows, smem=1, mib=16))
+    outs = [of(QUAD, MAIN, WIDE)] * 2 + [of(2, QUAD, MAIN, WIDE)] * (FAR - 1)
+    own, far, *pairs = call(select_kernel, outs, place, *rows, smem=1, mib=16)
+    return own, far, pairs
+
+
+def order(place, own, far, pairs, mate):
+    scratch = [pltpu.VMEM((EXPERTS, MAIN, D), bf16), pltpu.VMEM((EXPERTS, MAIN, HALF), bf16)]
+    args = (place, own, far, *pairs, mate)
+    outs = of(SLOT_ROWS + REST_ROWS, D)
+    return call(order_kernel, outs, *args, scratch=scratch, smem=1, mib=12)
 
 
 def dispatch(attended, masks):
@@ -297,20 +330,17 @@
     return call(hidden_kernel, of(TOK, D, dtype=f32), rows, residual, out_proj, mib=12)
 
 
-def experts(place, rows, out_proj, norm_gain, weights, slots):
+def experts(rows, residual, out_proj, norm_gain, weights):
     scratch = [
-        pltpu.VMEM((EXPERTS, MAIN, D), bf16),
-        pltpu.VMEM((EXPERTS, MAIN, HALF), bf16),
         pltpu.VMEM((SLOT_ROWS + REST_ROWS, D), bf16),
-        pltpu.VMEM((MODEL, D), bf16),
         pltpu.VMEM((D, FFW), bf16),
         pltpu.VMEM((D, FFW), bf16),
         pltpu.VMEM((FFW, D), bf16),
-        pltpu.SemaphoreType.DMA((4,)),
+        pltpu.SemaphoreType.DMA((3,)),
     ]
-    args = (rows, norm_gain.reshape(1, D), *slots, out_proj, *weights)
+    args = (rows, residual, out_proj, norm_gain.reshape(1, D), *weights)
     outs = of(SLOT_ROWS, WIDE)
-    return call(expert_kernel, outs, place, *args, scratch=scratch, smem=1, away=4, mib=50)
+    return call(expert_kernel, outs, *args, scratch=scratch, away=3, mib=51)
 
 
 def mix(rows, hidden, probs):
@@ -323,6 +353,15 @@
 
 def slots_exchange(x):
     return exchange(x.reshape(EXPERTS, MAIN, -1), ("y", "m")).reshape(SLOT_ROWS, -1)
+
+
+def shift_pairs(j):
+    pairs = []
+    for y in range(RING):
+        for m in range(QUAD):
+            to = (y + (j if m & 1 else -j)) % RING
+            pairs.append((y * QUAD + m, to * QUAD + m))
+    return pairs
 
 
 def layer(
@@ -332,20 +371,24 @@
     place = jnp.stack([lax.axis_index("y"), lax.axis_index("m")]).astype(i32)
     packed = pack(queries, keys, values)
     gathered = exchange(packed, "ctx")
-    rows = [stage(residual, routes)]
-    for other in range(1, QUAD):
-        rows.append(lax.ppermute(rows[0], "m", [(i, i ^ other) for i in range(QUAD)]))
-    slots = select(place, rows)
-    for shift in range(1, RING):
-        pairs = [(i, (i + shift) % RING) for i in range(RING)]
-        slots[shift] = lax.ppermute(slots[shift], "y", pairs)
+    mine = stage(residual, routes)
+    beside = lax.ppermute(mine, "m", [(i, i ^ 2) for i in range(QUAD)])
+    both = jnp.stack([mine, beside])
+    others = lax.ppermute(both, "m", [(i, i ^ 1) for i in range(QUAD)])
+    own, far, pairs = select(place, (mine, beside, others))
+    far = lax.ppermute(far, "y", [(i, (i + FAR) % RING) for i in range(RING)])
+    for j in range(1, FAR):
+        pairs[j - 1] = lax.ppermute(pairs[j - 1], ("y", "m"), shift_pairs(j))
     masks, probs = plan(routes, route_prob)
     attended = attend(part, gathered)
     attended = exchange(attended, "ctx")
     rows, x = dispatch(attended, masks)
     x = slots_exchange(x)
     hidden = hidden_of(rows, residual, out_proj)
-    x = experts(place, x, out_proj, norm_gain, (w_gate, w_up, w_down), slots)
+    mate = jnp.stack([pair[1] for pair in pairs])
+    mate = lax.ppermute(mate, "m", [(i, i ^ 1) for i in range(QUAD)])
+    ordered = order(place, own, far, pairs, mate)
+    x = experts(x, ordered, out_proj, norm_gain, (w_gate, w_up, w_down))
     x = slots_exchange(x)
     return mix(x, hidden, probs)
 

time: 224 us -> 216 us (0.964)
  starting transfers between devices: 78.2 us -> 66.2 us
    ppermute x10 -> x7, starting transfers between devices: 35.5 us -> 23.1 us  [the longest x3 11.6 us: layer(): pairs[j - 1] = lax.ppermute(pairs[j - 1], ('y', 'm'), shift_pairs(j))]
    ppermute x10 -> x7, waiting for transfers between devices: 38.6 us -> 46 us  [the longest x3 33.9 us: layer(): pairs[j - 1] = lax.ppermute(pairs[j - 1], ('y', 'm'), shift_pairs(j))]
    all_to_all x4, waiting for transfers between devices: 82.8 us -> 76.9 us  [exchange(): return lax.all_to_all(x, axes, split_axis=0, concat_axis=0, tiled=True)]
    pallas_call x9 -> x10, Pallas kernels: 20.7 us -> 21.7 us  [call(): pl.pallas_call(kernel, out_shape=outs, in_specs=specs + [pl.BlockSpec(mem...]
  transfers between devices with their start and end apart: 14 -> 11, of which waited for: 9 -> 7; matrix products, arithmetic and copies ran while one was open for 0% -> 0% of each run, Pallas kernels for 1% -> 4%
where the time goes in v4:
time: 216 us; the launch traced here: 215 us
  waiting for transfers between devices  123 us (57%)
  starting transfers between devices  66.2 us (31%)
  Pallas kernels  21.7 us (10%)
  local copies, waits for them, and re-layouts  4.06 us (2%)
    all_to_all x4, waiting for transfers between devices, exchange(): return lax.all_to_all(x, axes, split_axis=0, concat_axis=0, tiled=True)  76.9 us
    all_to_all x4, starting transfers between devices, exchange(): return lax.all_to_all(x, axes, split_axis=0, concat_axis=0, tiled=True)  43.1 us
    ppermute x3, waiting for transfers between devices, layer(): pairs[j - 1] = lax.ppermute(pairs[j - 1], ('y', 'm'), shift_pairs(j))  33.9 us
    pallas_call x10, Pallas kernels, call(): pl.pallas_call(kernel, out_shape=outs, in_specs=specs + [pl.BlockSpec(mem...  21.7 us
    ppermute x1, waiting for transfers between devices, layer(): far = lax.ppermute(far, 'y', [(i, (i + FAR) % RING) for i in range(RING)])  12 us
    ppermute x3, starting transfers between devices, layer(): pairs[j - 1] = lax.ppermute(pairs[j - 1], ('y', 'm'), shift_pairs(j))  11.6 us
  transfers between devices with their start and end apart: 11, of which 7 were waited for; matrix products, arithmetic and copies ran while one was open for 0% of the time, Pallas kernels for 4%

profile of v4, /device:TPU:1, one launch (start us, length us, event | category | flops | bytes accessed | tf_op | source)
XLA Modules:
  0.0 215.2 jit_solution(7059068257917661697)
XLA Ops:
  0.0 2.1 shard_map.109
  2.1 18.5 %all-to-all-start = ((bf16[24,152,128]{2,1,0:T(8,128)(2,1)}), bf16[24,152,128]{2,1,0:T(8,128)(2,1)S(1)}, u32[]{:S(2)}, u32[]{:S(2)}) async-start(bf16[24,152,128]{2,1,0:T(8,128)(2,1)} %shard_map.109), calls=%async_computation | async-start | bytes 1867776 | tf_op jit(solution)/shard_map/all_to_all | solution.py:351
  20.7 0.3 shard_map.113.refs_0_
  20.9 2.2 %collective-permute-start = (bf16[64,2176]{1,0:T(8,128)(2,1)S(1)}, bf16[64,2176]{1,0:T(8,128)(2,1)S(1)}, u32[]{:S(2)}, u32[]{:S(2)}) collective-permute-start(bf16[64,2176]{1,0:T(8,128)(2,1)S(1)} %shard_map.113.refs_0_), channel_id=1, source_target_pairs={{0,2},{1,3},{2,0},{3,1},{4,6},{5,7},{6,4},{7,5},{8,10},{9,11},{10,... | collective-permute-start | bytes 835592 | tf_op jit(solution)/shard_map/ppermute | solution.py:375
  23.2 32.6 %all-to-all-done.x_ref = bf16[24,152,128]{2,1,0:T(8,128)(2,1)S(1)} async-done(((bf16[24,152,128]{2,1,0:T(8,128)(2,1)}), bf16[24,152,128]{2,1,0:T(8,128)(2,1)S(1)}, u32[]{:S(2)}, u32[]{:S(2)}) %all-to-all-start) | async-done | bytes 933920 | tf_op jit(solution)/shard_map/all_to_all | solution.py:351
  55.8 2.4 %shard_map.110 = bf16[24,24,128]{2,1,0:T(8,128)(2,1)} custom-call(s32[1]{0:T(128)} %bitcast.part_ref, bf16[24,152,128]{2,1,0:T(8,128)(2,1)S(1)} %all-to-all-done.x_ref), custom_call_target="tpu_custom_call" | custom-call | tf_op jit(solution)/shard_map/pallas_call | solution.py:279
  58.2 8.0 %all-to-all-start.1 = ((bf16[24,24,128]{2,1,0:T(8,128)(2,1)}), bf16[24,24,128]{2,1,0:T(8,128)(2,1)S(1)}, u32[]{:S(2)}, u32[]{:S(2)}) async-start(bf16[24,24,128]{2,1,0:T(8,128)(2,1)} %shard_map.110), calls=%async_computation.1 | async-start | bytes 294912 | tf_op jit(solution)/shard_map/all_to_all | solution.py:351
  66.2 3.4 %collective-permute-start.1 = (bf16[2,64,2176]{2,1,0:T(8,128)(2,1)S(1)}, bf16[2,64,2176]{2,1,0:T(8,128)(2,1)S(1)}, u32[]{:S(2)}, u32[]{:S(2)}) collective-permute-start(bf16[2,64,2176]{2,1,0:T(8,128)(2,1)S(1)} %pad_maximum_fusion.1), channel_id=1, source_target_pairs={{0,1},{1,0},{2,3},{3,2},{4,5},{5,4},{6,7},{7,6},{8,9},{9,8},{10,11... | collective-permute-start | bytes 1671176 | tf_op jit(solution)/shard_map/ppermute | solution.py:377
  69.6 0.4 shard_map.111
  70.1 8.2 %all-to-all-done.1.a_ref = bf16[24,24,128]{2,1,0:T(8,128)(2,1)S(1)} async-done(((bf16[24,24,128]{2,1,0:T(8,128)(2,1)}), bf16[24,24,128]{2,1,0:T(8,128)(2,1)S(1)}, u32[]{:S(2)}, u32[]{:S(2)}) %all-to-all-start.1) | async-done | bytes 147488 | tf_op jit(solution)/shard_map/all_to_all | solution.py:351
  78.2 1.3 shard_map.112
  79.5 0.7 copy-done.3
  80.2 10.4 %all-to-all-start.2 = ((bf16[32,8,1536]{2,1,0:T(8,128)(2,1)}), bf16[32,8,1536]{2,1,0:T(8,128)(2,1)S(1)}, u32[]{:S(2)}, u32[]{:S(2)}) async-start(bf16[32,8,1536]{2,1,0:T(8,128)(2,1)} %bitcast.8), calls=%async_computation.2 | async-start | bytes 1572864 | tf_op jit(solution)/shard_map/all_to_all | solution.py:351
  90.6 0.1 pad_add_fusion.place_ref
  90.6 1.8 shard_map.114
  92.4 3.3 %collective-permute-start.3 = (bf16[2,4,8,3072]{3,2,1,0:T(8,128)(2,1)S(1)}, bf16[2,4,8,3072]{3,2,1,0:T(8,128)(2,1)S(1)}, u32[]{:S(2)}, u32[]{:S(2)}) collective-permute-start(bf16[2,4,8,3072]{3,2,1,0:T(8,128)(2,1)S(1)} %get-tuple-element.24), channel_id=1, source_target_pairs={{0,28},{1,5},{2,30},{3,7},{4,0},{5,9},{6,2},{7,11},{8,4},{9,13},{1... | collective-permute-start | bytes 1179656 | tf_op jit(solution)/shard_map/ppermute | solution.py:381
  95.7 4.0 %collective-permute-start.4 = (bf16[2,4,8,3072]{3,2,1,0:T(8,128)(2,1)S(1)}, bf16[2,4,8,3072]{3,2,1,0:T(8,128)(2,1)S(1)}, u32[]{:S(2)}, u32[]{:S(2)}) collective-permute-start(bf16[2,4,8,3072]{3,2,1,0:T(8,128)(2,1)S(1)} %get-tuple-element.25), channel_id=1, source_target_pairs={{0,24},{1,9},{2,26},{3,11},{4,28},{5,13},{6,30},{7,15},{8,0},{9,17... | collective-permute-start | bytes 1179656 | tf_op jit(solution)/shard_map/ppermute | solution.py:381
  99.7 4.4 %collective-permute-start.5 = (bf16[2,4,8,3072]{3,2,1,0:T(8,128)(2,1)S(1)}, bf16[2,4,8,3072]{3,2,1,0:T(8,128)(2,1)S(1)}, u32[]{:S(2)}, u32[]{:S(2)}) collective-permute-start(bf16[2,4,8,3072]{3,2,1,0:T(8,128)(2,1)S(1)} %get-tuple-element.26), channel_id=1, source_target_pairs={{0,20},{1,13},{2,22},{3,15},{4,24},{5,17},{6,26},{7,19},{8,28},{9,... | collective-permute-start | bytes 1179656 | tf_op jit(solution)/shard_map/ppermute | solution.py:381
  104.1 11.4 %collective-permute-done.3.refs_0_ = bf16[2,4,8,3072]{3,2,1,0:T(8,128)(2,1)S(1)} collective-permute-done((bf16[2,4,8,3072]{3,2,1,0:T(8,128)(2,1)S(1)}, bf16[2,4,8,3072]{3,2,1,0:T(8,128)(2,1)S(1)}, u32[]{:S(2)}, u32[]{:S(2)}) %collective-permute-start.3) | collective-permute-done | bytes 393248 | tf_op jit(solution)/shard_map/ppermute | solution.py:381
  115.5 6.9 %collective-permute-done.4.refs_1_ = bf16[2,4,8,3072]{3,2,1,0:T(8,128)(2,1)S(1)} collective-permute-done((bf16[2,4,8,3072]{3,2,1,0:T(8,128)(2,1)S(1)}, bf16[2,4,8,3072]{3,2,1,0:T(8,128)(2,1)S(1)}, u32[]{:S(2)}, u32[]{:S(2)}) %collective-permute-start.4) | collective-permute-done | bytes 393248 | tf_op jit(solution)/shard_map/ppermute | solution.py:381
  122.4 15.7 %collective-permute-done.5.refs_2_ = bf16[2,4,8,3072]{3,2,1,0:T(8,128)(2,1)S(1)} collective-permute-done((bf16[2,4,8,3072]{3,2,1,0:T(8,128)(2,1)S(1)}, bf16[2,4,8,3072]{3,2,1,0:T(8,128)(2,1)S(1)}, u32[]{:S(2)}, u32[]{:S(2)}) %collective-permute-start.5) | collective-permute-done | bytes 393248 | tf_op jit(solution)/shard_map/ppermute | solution.py:381
  138.2 1.9 collective-permute-start.6
  140.1 4.0 %collective-permute-start.2 = (bf16[4,8,3072]{2,1,0:T(8,128)(2,1)S(1)}, bf16[4,8,3072]{2,1,0:T(8,128)(2,1)S(1)}, u32[]{:S(2)}, u32[]{:S(2)}) collective-permute-start(bf16[4,8,3072]{2,1,0:T(8,128)(2,1)S(1)} %get-tuple-element.23), channel_id=1, source_target_pairs={{0,16},{4,20},{8,24},{12,28},{16,0},{20,4},{24,8},{28,12},{1,17},{... | collective-permute-start | bytes 589832 | tf_op jit(solution)/shard_map/ppermute | solution.py:379
  144.0 12.0 %collective-permute-done.2.far_ref = bf16[4,8,3072]{2,1,0:T(8,128)(2,1)S(1)} collective-permute-done((bf16[4,8,3072]{2,1,0:T(8,128)(2,1)S(1)}, bf16[4,8,3072]{2,1,0:T(8,128)(2,1)S(1)}, u32[]{:S(2)}, u32[]{:S(2)}) %collective-permute-start.2) | collective-permute-done | bytes 196640 | tf_op jit(solution)/shard_map/ppermute | solution.py:379
  156.1 1.0 shard_map.115.residual_ref
  157.1 1.2 copy-done.1
  158.3 9.5 %shard_map.116 = bf16[256,3072]{1,0:T(8,128)(2,1)} custom-call(bf16[256,1536]{1,0:T(8,128)(2,1)S(1)} %bitcast.25, bf16[384,2048]{1,0:T(8,128)(2,1)} %copy-done.1, bf16[1024,2048]{1,0:T(8,128)(2,1)} %w_ref.3, f32[1,2048]{1,0:T(1,128)S(1)} %bitcast.30, bf16[2048,512]{1,0:T(8,128)(2,1)} %bitcast.34, bf16[2048,512]{1,0:T(8,128)(2,1)} %bitcast.35, ...), custom_call_target="tpu_custom_call" | custom-call | tf_op jit(solution)/shard_map/pallas_call | solution.py:279
  167.8 6.2 %all-to-all-start.3 = ((bf16[32,8,3072]{2,1,0:T(8,128)(2,1)}), bf16[32,8,3072]{2,1,0:T(8,128)(2,1)S(1)}, u32[]{:S(2)}, u32[]{:S(2)}) async-start(bf16[32,8,3072]{2,1,0:T(8,128)(2,1)} %bitcast.20), calls=%async_computation.3 | async-start | bytes 3145728 | tf_op jit(solution)/shard_map/all_to_all | solution.py:351
  174.1 2.2 %copy-done = bf16[1024,2048]{1,0:T(8,128)(2,1)S(1)} copy-done((bf16[1024,2048]{1,0:T(8,128)(2,1)S(1)}, bf16[1024,2048]{1,0:T(8,128)(2,1)}, u32[]{:S(2)}) %copy-start) | copy-done | bytes 4194328
  176.3 0.8 shard_map.117.hidden_ref
  177.1 36.1 %all-to-all-done.3 = bf16[32,8,3072]{2,1,0:T(8,128)(2,1)S(1)} async-done(((bf16[32,8,3072]{2,1,0:T(8,128)(2,1)}), bf16[32,8,3072]{2,1,0:T(8,128)(2,1)S(1)}, u32[]{:S(2)}, u32[]{:S(2)}) %all-to-all-start.3) | async-done | bytes 1572896 | tf_op jit(solution)/shard_map/all_to_all | solution.py:351
  213.2 1.9 shard_map.118
  (22 shorter events, 0.2 us)
Async XLA Ops:
  0.0 20.7 %copy-start.6 = (s32[1,64,4]{1,2,0:T(4,128)S(1)}, s32[1,64,4]{1,2,0:T(4,128)}, u32[]{:S(2)}) copy-start(s32[1,64,4]{1,2,0:T(4,128)} %param.20) | copy-start | bytes 3076
  0.0 20.7 %copy-start.2 = (bf16[1,64,2048]{2,1,0:T(8,128)(2,1)S(1)}, bf16[1,64,2048]{2,1,0:T(8,128)(2,1)}, u32[]{:S(2)}) copy-start(bf16[1,64,2048]{2,1,0:T(8,128)(2,1)} %param.14) | copy-start | bytes 786436
  2.1 67.5 %copy-start.7 = (f32[1,64,4]{1,2,0:T(4,128)S(1)}, f32[1,64,4]{1,2,0:T(4,128)}, u32[]{:S(2)}) copy-start(f32[1,64,4]{1,2,0:T(4,128)} %param.21) | copy-start | bytes 3076
  2.1 53.6 %all-to-all-start = ((bf16[24,152,128]{2,1,0:T(8,128)(2,1)}), bf16[24,152,128]{2,1,0:T(8,128)(2,1)S(1)}, u32[]{:S(2)}, u32[]{:S(2)}) async-start(bf16[24,152,128]{2,1,0:T(8,128)(2,1)} %shard_map.109), calls=%async_computation | async-start | bytes 1867776 | tf_op jit(solution)/shard_map/all_to_all | solution.py:351
  20.9 45.2 %collective-permute-start = (bf16[64,2176]{1,0:T(8,128)(2,1)S(1)}, bf16[64,2176]{1,0:T(8,128)(2,1)S(1)}, u32[]{:S(2)}, u32[]{:S(2)}) collective-permute-start(bf16[64,2176]{1,0:T(8,128)(2,1)S(1)} %shard_map.113.refs_0_), channel_id=1, source_target_pairs={{0,2},{1,3},{2,0},{3,1},{4,6},{5,7},{6,4},{7,5},{8,10},{9,11},{10,... | collective-permute-start | bytes 835592 | tf_op jit(solution)/shard_map/ppermute | solution.py:375
  58.2 20.0 %all-to-all-start.1 = ((bf16[24,24,128]{2,1,0:T(8,128)(2,1)}), bf16[24,24,128]{2,1,0:T(8,128)(2,1)S(1)}, u32[]{:S(2)}, u32[]{:S(2)}) async-start(bf16[24,24,128]{2,1,0:T(8,128)(2,1)} %shard_map.110), calls=%async_computation.1 | async-start | bytes 294912 | tf_op jit(solution)/shard_map/all_to_all | solution.py:351
  66.2 24.4 %collective-permute-start.1 = (bf16[2,64,2176]{2,1,0:T(8,128)(2,1)S(1)}, bf16[2,64,2176]{2,1,0:T(8,128)(2,1)S(1)}, u32[]{:S(2)}, u32[]{:S(2)}) collective-permute-start(bf16[2,64,2176]{2,1,0:T(8,128)(2,1)S(1)} %pad_maximum_fusion.1), channel_id=1, source_target_pairs={{0,1},{1,0},{2,3},{3,2},{4,5},{5,4},{6,7},{7,6},{8,9},{9,8},{10,11... | collective-permute-start | bytes 1671176 | tf_op jit(solution)/shard_map/ppermute | solution.py:377
  79.5 0.7 copy-start.3
  80.2 78.1 %all-to-all-start.2 = ((bf16[32,8,1536]{2,1,0:T(8,128)(2,1)}), bf16[32,8,1536]{2,1,0:T(8,128)(2,1)S(1)}, u32[]{:S(2)}, u32[]{:S(2)}) async-start(bf16[32,8,1536]{2,1,0:T(8,128)(2,1)} %bitcast.8), calls=%async_computation.2 | async-start | bytes 1572864 | tf_op jit(solution)/shard_map/all_to_all | solution.py:351
  92.4 23.0 %collective-permute-start.3 = (bf16[2,4,8,3072]{3,2,1,0:T(8,128)(2,1)S(1)}, bf16[2,4,8,3072]{3,2,1,0:T(8,128)(2,1)S(1)}, u32[]{:S(2)}, u32[]{:S(2)}) collective-permute-start(bf16[2,4,8,3072]{3,2,1,0:T(8,128)(2,1)S(1)} %get-tuple-element.24), channel_id=1, source_target_pairs={{0,28},{1,5},{2,30},{3,7},{4,0},{5,9},{6,2},{7,11},{8,4},{9,13},{1... | collective-permute-start | bytes 1179656 | tf_op jit(solution)/shard_map/ppermute | solution.py:381
  95.7 26.7 %collective-permute-start.4 = (bf16[2,4,8,3072]{3,2,1,0:T(8,128)(2,1)S(1)}, bf16[2,4,8,3072]{3,2,1,0:T(8,128)(2,1)S(1)}, u32[]{:S(2)}, u32[]{:S(2)}) collective-permute-start(bf16[2,4,8,3072]{3,2,1,0:T(8,128)(2,1)S(1)} %get-tuple-element.25), channel_id=1, source_target_pairs={{0,24},{1,9},{2,26},{3,11},{4,28},{5,13},{6,30},{7,15},{8,0},{9,17... | collective-permute-start | bytes 1179656 | tf_op jit(solution)/shard_map/ppermute | solution.py:381
  99.7 38.4 %collective-permute-start.5 = (bf16[2,4,8,3072]{3,2,1,0:T(8,128)(2,1)S(1)}, bf16[2,4,8,3072]{3,2,1,0:T(8,128)(2,1)S(1)}, u32[]{:S(2)}, u32[]{:S(2)}) collective-permute-start(bf16[2,4,8,3072]{3,2,1,0:T(8,128)(2,1)S(1)} %get-tuple-element.26), channel_id=1, source_target_pairs={{0,20},{1,13},{2,22},{3,15},{4,24},{5,17},{6,26},{7,19},{8,28},{9,... | collective-permute-start | bytes 1179656 | tf_op jit(solution)/shard_map/ppermute | solution.py:381
  138.1 20.1 %copy-start.5 = (f32[2048]{0:T(1024)S(1)}, f32[2048]{0:T(1024)}, u32[]{:S(2)}) copy-start(f32[2048]{0:T(1024)} %param.16) | copy-start | bytes 24580
  138.2 17.9 %collective-permute-start.6 = (bf16[3,4,8,3072]{3,2,1,0:T(8,128)(2,1)S(1)}, bf16[3,4,8,3072]{3,2,1,0:T(8,128)(2,1)S(1)}, u32[]{:S(2)}, u32[]{:S(2)}) collective-permute-start(bf16[3,4,8,3072]{3,2,1,0:T(8,128)(2,1)S(1)} %pad_maximum_fusion), channel_id=1, source_target_pairs={{0,1},{1,0},{2,3},{3,2},{4,5},{5,4},{6,7},{7,6},{8,9},{9,8},{10,11... | collective-permute-start | bytes 1769480 | tf_op jit(solution)/shard_map/ppermute | solution.py:389
  140.1 16.0 %collective-permute-start.2 = (bf16[4,8,3072]{2,1,0:T(8,128)(2,1)S(1)}, bf16[4,8,3072]{2,1,0:T(8,128)(2,1)S(1)}, u32[]{:S(2)}, u32[]{:S(2)}) collective-permute-start(bf16[4,8,3072]{2,1,0:T(8,128)(2,1)S(1)} %get-tuple-element.23), channel_id=1, source_target_pairs={{0,16},{4,20},{8,24},{12,28},{16,0},{20,4},{24,8},{28,12},{1,17},{... | collective-permute-start | bytes 589832 | tf_op jit(solution)/shard_map/ppermute | solution.py:379
  157.1 1.2 copy-start.1
  167.8 6.3 %copy-start.4 = (bf16[64,1024]{1,0:T(8,128)(2,1)S(1)}, bf16[64,1024]{1,0:T(8,128)(2,1)}, u32[]{:S(2)}) copy-start(bf16[64,1024]{1,0:T(8,128)(2,1)} %copy-done.3) | copy-start | bytes 393220
  167.8 45.4 %all-to-all-start.3 = ((bf16[32,8,3072]{2,1,0:T(8,128)(2,1)}), bf16[32,8,3072]{2,1,0:T(8,128)(2,1)S(1)}, u32[]{:S(2)}, u32[]{:S(2)}) async-start(bf16[32,8,3072]{2,1,0:T(8,128)(2,1)} %bitcast.20), calls=%async_computation.3 | async-start | bytes 3145728 | tf_op jit(solution)/shard_map/all_to_all | solution.py:351
  174.1 2.2 %copy-start = (bf16[1024,2048]{1,0:T(8,128)(2,1)S(1)}, bf16[1024,2048]{1,0:T(8,128)(2,1)}, u32[]{:S(2)}) copy-start(bf16[1024,2048]{1,0:T(8,128)(2,1)} %w_ref.3) | copy-start | bytes 12582916

commit v5 on v4

--- a/solution.py
+++ b/solution.py
@@ -11,13 +11,12 @@
 TOP = 4
 TOK = 64
 D = 2048
-FFW = 512
 N_CTX = 24
 EXPERTS = 32
 PARTS = N_CTX // HEADS
 Q_ROWS = 24
 CHUNK = 2 * TOK + Q_ROWS
-GROUP = 6
+GROUP = 8
 MAIN = 8
 REST = 4
 HALF = D // 2
@@ -192,12 +191,13 @@
     masks = masks_of(dot(spread, slots_of(routes).astype(bf16)))
     for mask, out in zip(masks, outs[:3]):
         out[...] = mask.astype(bf16)
-    for term in range(3):
-        part = prob.astype(bf16)
-        prob = prob - part.astype(f32)
-        wide = dot(spread, part)
-        for mask, out in zip(masks, outs[3:]):
-            out[term] = jnp.where(mask, wide, 0.0).astype(bf16)
+    terms = []
+    for _ in range(3):
+        terms.append(prob.astype(bf16))
+        prob = prob - terms[-1].astype(f32)
+    wide = [dot(spread, term) for term in terms]
+    for mask, out in zip(masks, outs[3:]):
+        out[...] = jnp.concatenate([jnp.where(mask, w, 0.0) for w in wide], axis=1).astype(bf16)
 
 
 def dispatch_kernel(a_ref, m_ref, l_ref, h_ref, rows_ref, o_ref):
@@ -218,40 +218,45 @@
     o_ref[...] = residual_ref[...].astype(f32) + dot(rows_ref[...], w_ref[...])
 
 
-def normed_of(residual, attended, w_ref, gain_ref):
-    hidden = residual.astype(f32) + dot(attended, w_ref[...])
-    mean_square = jnp.mean(hidden * hidden, axis=-1, keepdims=True)
-    return (hidden * lax.rsqrt(mean_square + 1e-05) * gain_ref[...]).astype(bf16)
-
-
 def picker(high):
     row = lax.broadcasted_iota(jnp.int32, (REST_ROWS, SLOT_ROWS), 0)
     col = lax.broadcasted_iota(jnp.int32, (REST_ROWS, SLOT_ROWS), 1)
     return (col == (row >> 2) * MAIN + (row & 3) + (REST if high else 0)).astype(bf16)
 
 
-def expert_kernel(x_ref, residual_ref, w_ref, gain_ref, *refs):
-    weights, (o_ref, rows_ref, *held, sems) = refs[:3], refs[3:]
-    gate_ref, up_ref, down_ref = held
+def expert_kernel(x_ref, residual_ref, gain_ref, *refs):
+    weights, (o_ref, rows_ref, hidden_ref, w_ref, gate_ref, up_ref, down_ref, sems) = refs[:4], refs[4:]
+    halves = (slice(0, HALF), slice(HALF, D))
+    pairs = [(weights[0].at[:, cols], w_ref.at[:, cols]) for cols in halves]
+    pairs += list(zip(weights[1:], (gate_ref, up_ref, down_ref)))
     copies = [
         pltpu.make_async_copy(source, target, sems.at[i])
-        for i, (source, target) in enumerate(zip(weights, held))
+        for i, (source, target) in enumerate(pairs)
     ]
     for copy in copies:
         copy.start()
     low, high = picker(False), picker(True)
     main = slice(0, SLOT_ROWS)
     rest = slice(SLOT_ROWS, SLOT_ROWS + REST_ROWS)
-    rows_ref[main, :] = normed_of(residual_ref[main, :], x_ref[:, 0:MODEL], w_ref, gain_ref)
-    halves = x_ref[:, MODEL:WIDE_MODEL]
-    attended = jnp.concatenate([dot(low, halves), dot(high, halves)], axis=1).astype(bf16)
-    rows_ref[rest, :] = normed_of(residual_ref[rest, :], attended, w_ref, gain_ref)
-    copies[0].wait()
+    tail = x_ref[:, MODEL:WIDE_MODEL]
+    tail = jnp.concatenate([dot(low, tail), dot(high, tail)], axis=1).astype(bf16)
+    attended = ((main, x_ref[:, 0:MODEL]), (rest, tail))
+    squares = [0.0, 0.0]
+    for copy, cols in zip(copies, halves):
+        copy.wait()
+        for i, (rows, have) in enumerate(attended):
+            hidden = residual_ref[rows, cols].astype(f32) + dot(have, w_ref[:, cols])
+            squares[i] += jnp.sum(hidden * hidden, axis=-1, keepdims=True)
+            hidden_ref[rows, cols] = hidden
+    for (rows, _), square in zip(attended, squares):
+        factor = lax.rsqrt(square * (1.0 / D) + 1e-05)
+        rows_ref[rows, :] = (hidden_ref[rows, :] * factor * gain_ref[...]).astype(bf16)
+    copies[2].wait()
     gate = dot(rows_ref[...], gate_ref[...])
-    copies[1].wait()
+    copies[3].wait()
     up = dot(rows_ref[...], up_ref[...])
     act = (gate / (1.0 + jnp.exp(-gate)) * up).astype(bf16)
-    copies[2].wait()
+    copies[4].wait()
     made = dot(act, down_ref[...]).astype(bf16)
     o_ref[:, 0:D] = made[main]
     o_ref[:, D:WIDE] = (
@@ -260,16 +265,14 @@
 
 
 def mix_kernel(y_ref, hidden_ref, m_ref, l_ref, h_ref, o_ref):
-    total = hidden_ref[...]
+    def terms(p_ref, rows):
+        made = dot_first(p_ref[...], rows)
+        return made[0:TOK] + made[TOK : 2 * TOK] + made[2 * TOK :]
+
+    total = hidden_ref[...] + terms(m_ref, y_ref[:, 0:D])
     rest = y_ref[:, D:WIDE]
-    first = jnp.zeros((TOK, HALF), f32)
-    second = jnp.zeros((TOK, HALF), f32)
-    for term in range(3):
-        total = total + dot_first(m_ref[term], y_ref[:, 0:D])
-        first = first + dot_first(l_ref[term], rest)
-        second = second + dot_first(h_ref[term], rest)
-    o_ref[:, 0:HALF] = (total[:, 0:HALF] + first).astype(bf16)
-    o_ref[:, HALF:D] = (total[:, HALF:D] + second).astype(bf16)
+    o_ref[:, 0:HALF] = (total[:, 0:HALF] + terms(l_ref, rest)).astype(bf16)
+    o_ref[:, HALF:D] = (total[:, HALF:D] + terms(h_ref, rest)).astype(bf16)
 
 
 def call(kernel, outs, *args, scratch=(), smem=0, away=0, mib=16):
@@ -299,7 +302,7 @@
 
 
 def plan(routes, prob):
-    outs = [of(SLOT_ROWS, TOK)] * 3 + [of(3, SLOT_ROWS, TOK)] * 3
+    outs = [of(SLOT_ROWS, TOK)] * 3 + [of(SLOT_ROWS, 3 * TOK)] * 3
     made = call(plan_kernel, outs, routes.T, prob.T, mib=8)
     return made[:3], made[3:]
 
@@ -330,17 +333,16 @@
     return call(hidden_kernel, of(TOK, D, dtype=f32), rows, residual, out_proj, mib=12)
 
 
-def experts(rows, residual, out_proj, norm_gain, weights):
+def experts(rows, residual, norm_gain, weights):
     scratch = [
         pltpu.VMEM((SLOT_ROWS + REST_ROWS, D), bf16),
-        pltpu.VMEM((D, FFW), bf16),
-        pltpu.VMEM((D, FFW), bf16),
-        pltpu.VMEM((FFW, D), bf16),
-        pltpu.SemaphoreType.DMA((3,)),
+        pltpu.VMEM((SLOT_ROWS + REST_ROWS, D), f32),
+        *[pltpu.VMEM(w.shape, bf16) for w in weights],
+        pltpu.SemaphoreType.DMA((5,)),
     ]
-    args = (rows, residual, out_proj, norm_gain.reshape(1, D), *weights)
+    args = (rows, residual, norm_gain.reshape(1, D), *weights)
     outs = of(SLOT_ROWS, WIDE)
-    return call(expert_kernel, outs, *args, scratch=scratch, away=3, mib=51)
+    return call(expert_kernel, outs, *args, scratch=scratch, away=4, mib=50)
 
 
 def mix(rows, hidden, probs):
@@ -388,7 +390,7 @@
     mate = jnp.stack([pair[1] for pair in pairs])
     mate = lax.ppermute(mate, "m", [(i, i ^ 1) for i in range(QUAD)])
     ordered = order(place, own, far, pairs, mate)
-    x = experts(x, ordered, out_proj, norm_gain, (w_gate, w_up, w_down))
+    x = experts(x, ordered, norm_gain, (out_proj, w_gate, w_up, w_down))
     x = slots_exchange(x)
     return mix(x, hidden, probs)
 

time: 216 us -> 212 us (0.981)
  transfers between devices with their start and end apart: 11 -> 11, of which waited for: 7 -> 7; matrix products, arithmetic and copies ran while one was open for 0% -> 1% of each run, Pallas kernels for 4% -> 4%
where the time goes in v5:
time: 212 us; the launch traced here: 211 us
  waiting for transfers between devices  122 us (58%)
  starting transfers between devices  66 us (31%)
  Pallas kernels  19.8 us (9%)
  local copies, waits for them, and re-layouts  2.24 us (1%)
    all_to_all x4, waiting for transfers between devices, exchange(): return lax.all_to_all(x, axes, split_axis=0, concat_axis=0, tiled=True)  76 us
    all_to_all x4, starting transfers between devices, exchange(): return lax.all_to_all(x, axes, split_axis=0, concat_axis=0, tiled=True)  42.9 us
    ppermute x3, waiting for transfers between devices, layer(): pairs[j - 1] = lax.ppermute(pairs[j - 1], ('y', 'm'), shift_pairs(j))  34 us
    pallas_call x10, Pallas kernels, call(): pl.pallas_call(kernel, out_shape=outs, in_specs=specs + [pl.BlockSpec(mem...  19.8 us
    ppermute x1, waiting for transfers between devices, layer(): far = lax.ppermute(far, 'y', [(i, (i + FAR) % RING) for i in range(RING)])  12 us
    ppermute x3, starting transfers between devices, layer(): pairs[j - 1] = lax.ppermute(pairs[j - 1], ('y', 'm'), shift_pairs(j))  11.6 us
  transfers between devices with their start and end apart: 11, of which 7 were waited for; matrix products, arithmetic and copies ran while one was open for 1% of the time, Pallas kernels for 4%

profile of v5, /device:TPU:1, one launch (start us, length us, event | category | flops | bytes accessed | tf_op | source)
XLA Modules:
  0.0 211.4 jit_solution(2420394608231068937)
XLA Ops:
  0.0 2.1 %shard_map.109 = bf16[24,152,128]{2,1,0:T(8,128)(2,1)} custom-call(bf16[64,1024]{1,0:T(8,128)(2,1)} %bitcast.37, bf16[64,1024]{1,0:T(8,128)(2,1)} %bitcast.38, bf16[64,1024]{1,0:T(8,128)(2,1)} %bitcast.39), custom_call_target="tpu_custom_call" | custom-call | tf_op jit(solution)/shard_map/pallas_call | solution.py:282
  2.1 18.5 %all-to-all-start = ((bf16[24,152,128]{2,1,0:T(8,128)(2,1)}), bf16[24,152,128]{2,1,0:T(8,128)(2,1)S(1)}, u32[]{:S(2)}, u32[]{:S(2)}) async-start(bf16[24,152,128]{2,1,0:T(8,128)(2,1)} %shard_map.109), calls=%async_computation | async-start | bytes 1867776 | tf_op jit(solution)/shard_map/all_to_all | solution.py:353
  20.7 0.3 shard_map.113.refs_0_
  20.9 2.2 %collective-permute-start = (bf16[64,2176]{1,0:T(8,128)(2,1)S(1)}, bf16[64,2176]{1,0:T(8,128)(2,1)S(1)}, u32[]{:S(2)}, u32[]{:S(2)}) collective-permute-start(bf16[64,2176]{1,0:T(8,128)(2,1)S(1)} %shard_map.113.refs_0_), channel_id=1, source_target_pairs={{0,2},{1,3},{2,0},{3,1},{4,6},{5,7},{6,4},{7,5},{8,10},{9,11},{10,... | collective-permute-start | bytes 835592 | tf_op jit(solution)/shard_map/ppermute | solution.py:377
  23.2 32.6 %all-to-all-done.x_ref = bf16[24,152,128]{2,1,0:T(8,128)(2,1)S(1)} async-done(((bf16[24,152,128]{2,1,0:T(8,128)(2,1)}), bf16[24,152,128]{2,1,0:T(8,128)(2,1)S(1)}, u32[]{:S(2)}, u32[]{:S(2)}) %all-to-all-start) | async-done | bytes 933920 | tf_op jit(solution)/shard_map/all_to_all | solution.py:353
  55.8 2.1 shard_map.110
  57.9 8.0 %all-to-all-start.1 = ((bf16[24,24,128]{2,1,0:T(8,128)(2,1)}), bf16[24,24,128]{2,1,0:T(8,128)(2,1)S(1)}, u32[]{:S(2)}, u32[]{:S(2)}) async-start(bf16[24,24,128]{2,1,0:T(8,128)(2,1)} %shard_map.110), calls=%async_computation.1 | async-start | bytes 294912 | tf_op jit(solution)/shard_map/all_to_all | solution.py:353
  65.8 0.9 pad_maximum_fusion.1
  66.7 3.4 %collective-permute-start.1 = (bf16[2,64,2176]{2,1,0:T(8,128)(2,1)}, bf16[2,64,2176]{2,1,0:T(8,128)(2,1)S(1)}, u32[]{:S(2)}, u32[]{:S(2)}) collective-permute-start(bf16[2,64,2176]{2,1,0:T(8,128)(2,1)} %pad_maximum_fusion.1), channel_id=1, source_target_pairs={{0,1},{1,0},{2,3},{3,2},{4,5},{5,4},{6,7},{7,6},{8,9},{9,8},{10,11... | collective-permute-start | bytes 1671176 | tf_op jit(solution)/shard_map/ppermute | solution.py:379
  70.1 0.5 shard_map.111
  70.6 7.3 %all-to-all-done.1.a_ref = bf16[24,24,128]{2,1,0:T(8,128)(2,1)S(1)} async-done(((bf16[24,24,128]{2,1,0:T(8,128)(2,1)}), bf16[24,24,128]{2,1,0:T(8,128)(2,1)S(1)}, u32[]{:S(2)}, u32[]{:S(2)}) %all-to-all-start.1) | async-done | bytes 147488 | tf_op jit(solution)/shard_map/all_to_all | solution.py:353
  77.9 1.3 shard_map.112
  79.2 10.4 %all-to-all-start.2 = ((bf16[32,8,1536]{2,1,0:T(8,128)(2,1)}), bf16[32,8,1536]{2,1,0:T(8,128)(2,1)S(1)}, u32[]{:S(2)}, u32[]{:S(2)}) async-start(bf16[32,8,1536]{2,1,0:T(8,128)(2,1)} %bitcast.8), calls=%async_computation.2 | async-start | bytes 1572864 | tf_op jit(solution)/shard_map/all_to_all | solution.py:353
  89.6 0.1 pad_add_fusion.place_ref
  89.7 1.7 shard_map.114
  91.4 3.2 %collective-permute-start.3 = (bf16[2,4,8,3072]{3,2,1,0:T(8,128)(2,1)S(1)}, bf16[2,4,8,3072]{3,2,1,0:T(8,128)(2,1)S(1)}, u32[]{:S(2)}, u32[]{:S(2)}) collective-permute-start(bf16[2,4,8,3072]{3,2,1,0:T(8,128)(2,1)S(1)} %get-tuple-element.24), channel_id=1, source_target_pairs={{0,28},{1,5},{2,30},{3,7},{4,0},{5,9},{6,2},{7,11},{8,4},{9,13},{1... | collective-permute-start | bytes 1179656 | tf_op jit(solution)/shard_map/ppermute | solution.py:383
  94.7 4.0 %collective-permute-start.4 = (bf16[2,4,8,3072]{3,2,1,0:T(8,128)(2,1)S(1)}, bf16[2,4,8,3072]{3,2,1,0:T(8,128)(2,1)S(1)}, u32[]{:S(2)}, u32[]{:S(2)}) collective-permute-start(bf16[2,4,8,3072]{3,2,1,0:T(8,128)(2,1)S(1)} %get-tuple-element.25), channel_id=1, source_target_pairs={{0,24},{1,9},{2,26},{3,11},{4,28},{5,13},{6,30},{7,15},{8,0},{9,17... | collective-permute-start | bytes 1179656 | tf_op jit(solution)/shard_map/ppermute | solution.py:383
  98.7 4.3 %collective-permute-start.5 = (bf16[2,4,8,3072]{3,2,1,0:T(8,128)(2,1)S(1)}, bf16[2,4,8,3072]{3,2,1,0:T(8,128)(2,1)S(1)}, u32[]{:S(2)}, u32[]{:S(2)}) collective-permute-start(bf16[2,4,8,3072]{3,2,1,0:T(8,128)(2,1)S(1)} %get-tuple-element.26), channel_id=1, source_target_pairs={{0,20},{1,13},{2,22},{3,15},{4,24},{5,17},{6,26},{7,19},{8,28},{9,... | collective-permute-start | bytes 1179656 | tf_op jit(solution)/shard_map/ppermute | solution.py:383
  103.1 11.4 %collective-permute-done.3.refs_0_ = bf16[2,4,8,3072]{3,2,1,0:T(8,128)(2,1)S(1)} collective-permute-done((bf16[2,4,8,3072]{3,2,1,0:T(8,128)(2,1)S(1)}, bf16[2,4,8,3072]{3,2,1,0:T(8,128)(2,1)S(1)}, u32[]{:S(2)}, u32[]{:S(2)}) %collective-permute-start.3) | collective-permute-done | bytes 393248 | tf_op jit(solution)/shard_map/ppermute | solution.py:383
  114.5 6.9 %collective-permute-done.4.refs_1_ = bf16[2,4,8,3072]{3,2,1,0:T(8,128)(2,1)S(1)} collective-permute-done((bf16[2,4,8,3072]{3,2,1,0:T(8,128)(2,1)S(1)}, bf16[2,4,8,3072]{3,2,1,0:T(8,128)(2,1)S(1)}, u32[]{:S(2)}, u32[]{:S(2)}) %collective-permute-start.4) | collective-permute-done | bytes 393248 | tf_op jit(solution)/shard_map/ppermute | solution.py:383
  121.4 15.7 %collective-permute-done.5.refs_2_ = bf16[2,4,8,3072]{3,2,1,0:T(8,128)(2,1)S(1)} collective-permute-done((bf16[2,4,8,3072]{3,2,1,0:T(8,128)(2,1)S(1)}, bf16[2,4,8,3072]{3,2,1,0:T(8,128)(2,1)S(1)}, u32[]{:S(2)}, u32[]{:S(2)}) %collective-permute-start.5) | collective-permute-done | bytes 393248 | tf_op jit(solution)/shard_map/ppermute | solution.py:383
  137.1 0.1 pad_maximum_fusion
  137.2 1.9 collective-permute-start.6
  139.1 4.0 %collective-permute-start.2 = (bf16[4,8,3072]{2,1,0:T(8,128)(2,1)S(1)}, bf16[4,8,3072]{2,1,0:T(8,128)(2,1)S(1)}, u32[]{:S(2)}, u32[]{:S(2)}) collective-permute-start(bf16[4,8,3072]{2,1,0:T(8,128)(2,1)S(1)} %get-tuple-element.23), channel_id=1, source_target_pairs={{0,16},{4,20},{8,24},{12,28},{16,0},{20,4},{24,8},{28,12},{1,17},{... | collective-permute-start | bytes 589832 | tf_op jit(solution)/shard_map/ppermute | solution.py:381
  143.1 12.0 %collective-permute-done.2.far_ref = bf16[4,8,3072]{2,1,0:T(8,128)(2,1)S(1)} collective-permute-done((bf16[4,8,3072]{2,1,0:T(8,128)(2,1)S(1)}, bf16[4,8,3072]{2,1,0:T(8,128)(2,1)S(1)}, u32[]{:S(2)}, u32[]{:S(2)}) %collective-permute-start.2) | collective-permute-done | bytes 196640 | tf_op jit(solution)/shard_map/ppermute | solution.py:381
  155.1 1.0 shard_map.115.residual_ref
  156.1 8.6 %shard_map.116 = bf16[256,3072]{1,0:T(8,128)(2,1)} custom-call(bf16[256,1536]{1,0:T(8,128)(2,1)S(1)} %bitcast.25, bf16[384,2048]{1,0:T(8,128)(2,1)S(1)} %shard_map.115.residual_ref, f32[1,2048]{1,0:T(1,128)S(1)} %bitcast.30, bf16[1024,2048]{1,0:T(8,128)(2,1)} %w_ref.1, bf16[2048,512]{1,0:T(8,128)(2,1)} %bitcast.34, bf16[2048,512]{1,0:T(8,128)(2,1)} %bitcast.35, ...), custom_call_target="tpu_custom_call" | custom-call | tf_op jit(solution)/shard_map/pallas_call | solution.py:282
  164.8 6.1 %all-to-all-start.3 = ((bf16[32,8,3072]{2,1,0:T(8,128)(2,1)}), bf16[32,8,3072]{2,1,0:T(8,128)(2,1)S(1)}, u32[]{:S(2)}, u32[]{:S(2)}) async-start(bf16[32,8,3072]{2,1,0:T(8,128)(2,1)} %bitcast.20), calls=%async_computation.3 | async-start | bytes 3145728 | tf_op jit(solution)/shard_map/all_to_all | solution.py:353
  170.9 2.2 %copy-done = bf16[1024,2048]{1,0:T(8,128)(2,1)S(1)} copy-done((bf16[1024,2048]{1,0:T(8,128)(2,1)S(1)}, bf16[1024,2048]{1,0:T(8,128)(2,1)}, u32[]{:S(2)}) %copy-start) | copy-done | bytes 4194328
  173.1 0.8 shard_map.117.hidden_ref
  173.9 36.1 %all-to-all-done.3 = bf16[32,8,3072]{2,1,0:T(8,128)(2,1)S(1)} async-done(((bf16[32,8,3072]{2,1,0:T(8,128)(2,1)}), bf16[32,8,3072]{2,1,0:T(8,128)(2,1)S(1)}, u32[]{:S(2)}, u32[]{:S(2)}) %all-to-all-start.3) | async-done | bytes 1572896 | tf_op jit(solution)/shard_map/all_to_all | solution.py:353
  210.1 1.3 shard_map.118
  (16 shorter events, 0.1 us)
Async XLA Ops:
  0.0 20.7 %copy-start.3 = (s32[1,64,4]{1,2,0:T(4,128)S(1)}, s32[1,64,4]{1,2,0:T(4,128)}, u32[]{:S(2)}) copy-start(s32[1,64,4]{1,2,0:T(4,128)} %param.20) | copy-start | bytes 3076
  0.0 20.7 %copy-start.1 = (bf16[1,64,2048]{2,1,0:T(8,128)(2,1)S(1)}, bf16[1,64,2048]{2,1,0:T(8,128)(2,1)}, u32[]{:S(2)}) copy-start(bf16[1,64,2048]{2,1,0:T(8,128)(2,1)} %param.14) | copy-start | bytes 786436
  2.1 67.9 %copy-start.4 = (f32[1,64,4]{1,2,0:T(4,128)S(1)}, f32[1,64,4]{1,2,0:T(4,128)}, u32[]{:S(2)}) copy-start(f32[1,64,4]{1,2,0:T(4,128)} %param.21) | copy-start | bytes 3076
  2.1 53.6 %all-to-all-start = ((bf16[24,152,128]{2,1,0:T(8,128)(2,1)}), bf16[24,152,128]{2,1,0:T(8,128)(2,1)S(1)}, u32[]{:S(2)}, u32[]{:S(2)}) async-start(bf16[24,152,128]{2,1,0:T(8,128)(2,1)} %shard_map.109), calls=%async_computation | async-start | bytes 1867776 | tf_op jit(solution)/shard_map/all_to_all | solution.py:353
  20.9 44.9 %collective-permute-start = (bf16[64,2176]{1,0:T(8,128)(2,1)S(1)}, bf16[64,2176]{1,0:T(8,128)(2,1)S(1)}, u32[]{:S(2)}, u32[]{:S(2)}) collective-permute-start(bf16[64,2176]{1,0:T(8,128)(2,1)S(1)} %shard_map.113.refs_0_), channel_id=1, source_target_pairs={{0,2},{1,3},{2,0},{3,1},{4,6},{5,7},{6,4},{7,5},{8,10},{9,11},{10,... | collective-permute-start | bytes 835592 | tf_op jit(solution)/shard_map/ppermute | solution.py:377
  57.9 20.0 %all-to-all-start.1 = ((bf16[24,24,128]{2,1,0:T(8,128)(2,1)}), bf16[24,24,128]{2,1,0:T(8,128)(2,1)S(1)}, u32[]{:S(2)}, u32[]{:S(2)}) async-start(bf16[24,24,128]{2,1,0:T(8,128)(2,1)} %shard_map.110), calls=%async_computation.1 | async-start | bytes 294912 | tf_op jit(solution)/shard_map/all_to_all | solution.py:353
  66.7 23.0 %collective-permute-start.1 = (bf16[2,64,2176]{2,1,0:T(8,128)(2,1)}, bf16[2,64,2176]{2,1,0:T(8,128)(2,1)S(1)}, u32[]{:S(2)}, u32[]{:S(2)}) collective-permute-start(bf16[2,64,2176]{2,1,0:T(8,128)(2,1)} %pad_maximum_fusion.1), channel_id=1, source_target_pairs={{0,1},{1,0},{2,3},{3,2},{4,5},{5,4},{6,7},{7,6},{8,9},{9,8},{10,11... | collective-permute-start | bytes 1671176 | tf_op jit(solution)/shard_map/ppermute | solution.py:379
  79.2 76.9 %all-to-all-start.2 = ((bf16[32,8,1536]{2,1,0:T(8,128)(2,1)}), bf16[32,8,1536]{2,1,0:T(8,128)(2,1)S(1)}, u32[]{:S(2)}, u32[]{:S(2)}) async-start(bf16[32,8,1536]{2,1,0:T(8,128)(2,1)} %bitcast.8), calls=%async_computation.2 | async-start | bytes 1572864 | tf_op jit(solution)/shard_map/all_to_all | solution.py:353
  91.4 23.1 %collective-permute-start.3 = (bf16[2,4,8,3072]{3,2,1,0:T(8,128)(2,1)S(1)}, bf16[2,4,8,3072]{3,2,1,0:T(8,128)(2,1)S(1)}, u32[]{:S(2)}, u32[]{:S(2)}) collective-permute-start(bf16[2,4,8,3072]{3,2,1,0:T(8,128)(2,1)S(1)} %get-tuple-element.24), channel_id=1, source_target_pairs={{0,28},{1,5},{2,30},{3,7},{4,0},{5,9},{6,2},{7,11},{8,4},{9,13},{1... | collective-permute-start | bytes 1179656 | tf_op jit(solution)/shard_map/ppermute | solution.py:383
  94.7 26.7 %collective-permute-start.4 = (bf16[2,4,8,3072]{3,2,1,0:T(8,128)(2,1)S(1)}, bf16[2,4,8,3072]{3,2,1,0:T(8,128)(2,1)S(1)}, u32[]{:S(2)}, u32[]{:S(2)}) collective-permute-start(bf16[2,4,8,3072]{3,2,1,0:T(8,128)(2,1)S(1)} %get-tuple-element.25), channel_id=1, source_target_pairs={{0,24},{1,9},{2,26},{3,11},{4,28},{5,13},{6,30},{7,15},{8,0},{9,17... | collective-permute-start | bytes 1179656 | tf_op jit(solution)/shard_map/ppermute | solution.py:383
  98.7 38.3 %collective-permute-start.5 = (bf16[2,4,8,3072]{3,2,1,0:T(8,128)(2,1)S(1)}, bf16[2,4,8,3072]{3,2,1,0:T(8,128)(2,1)S(1)}, u32[]{:S(2)}, u32[]{:S(2)}) collective-permute-start(bf16[2,4,8,3072]{3,2,1,0:T(8,128)(2,1)S(1)} %get-tuple-element.26), channel_id=1, source_target_pairs={{0,20},{1,13},{2,22},{3,15},{4,24},{5,17},{6,26},{7,19},{8,28},{9,... | collective-permute-start | bytes 1179656 | tf_op jit(solution)/shard_map/ppermute | solution.py:383
  137.2 19.0 %copy-start.2 = (f32[2048]{0:T(1024)S(1)}, f32[2048]{0:T(1024)}, u32[]{:S(2)}) copy-start(f32[2048]{0:T(1024)} %param.16) | copy-start | bytes 24580
  137.2 17.9 %collective-permute-start.6 = (bf16[3,4,8,3072]{3,2,1,0:T(8,128)(2,1)S(1)}, bf16[3,4,8,3072]{3,2,1,0:T(8,128)(2,1)S(1)}, u32[]{:S(2)}, u32[]{:S(2)}) collective-permute-start(bf16[3,4,8,3072]{3,2,1,0:T(8,128)(2,1)S(1)} %pad_maximum_fusion), channel_id=1, source_target_pairs={{0,1},{1,0},{2,3},{3,2},{4,5},{5,4},{6,7},{7,6},{8,9},{9,8},{10,11... | collective-permute-start | bytes 1769480 | tf_op jit(solution)/shard_map/ppermute | solution.py:391
  139.1 16.0 %collective-permute-start.2 = (bf16[4,8,3072]{2,1,0:T(8,128)(2,1)S(1)}, bf16[4,8,3072]{2,1,0:T(8,128)(2,1)S(1)}, u32[]{:S(2)}, u32[]{:S(2)}) collective-permute-start(bf16[4,8,3072]{2,1,0:T(8,128)(2,1)S(1)} %get-tuple-element.23), channel_id=1, source_target_pairs={{0,16},{4,20},{8,24},{12,28},{16,0},{20,4},{24,8},{28,12},{1,17},{... | collective-permute-start | bytes 589832 | tf_op jit(solution)/shard_map/ppermute | solution.py:381
  164.8 45.3 %all-to-all-start.3 = ((bf16[32,8,3072]{2,1,0:T(8,128)(2,1)}), bf16[32,8,3072]{2,1,0:T(8,128)(2,1)S(1)}, u32[]{:S(2)}, u32[]{:S(2)}) async-start(bf16[32,8,3072]{2,1,0:T(8,128)(2,1)} %bitcast.20), calls=%async_computation.3 | async-start | bytes 3145728 | tf_op jit(solution)/shard_map/all_to_all | solution.py:353
  170.9 2.2 %copy-start = (bf16[1024,2048]{1,0:T(8,128)(2,1)S(1)}, bf16[1024,2048]{1,0:T(8,128)(2,1)}, u32[]{:S(2)}) copy-start(bf16[1024,2048]{1,0:T(8,128)(2,1)} %w_ref.1) | copy-start | bytes 12582916

commit v6 on v5

--- a/solution.py
+++ b/solution.py
@@ -228,7 +228,8 @@
     weights, (o_ref, rows_ref, hidden_ref, w_ref, gate_ref, up_ref, down_ref, sems) = refs[:4], refs[4:]
     halves = (slice(0, HALF), slice(HALF, D))
     pairs = [(weights[0].at[:, cols], w_ref.at[:, cols]) for cols in halves]
-    pairs += list(zip(weights[1:], (gate_ref, up_ref, down_ref)))
+    pairs += list(zip(weights[1:3], (gate_ref, up_ref)))
+    pairs += [(weights[3].at[:, cols], down_ref.at[:, cols]) for cols in halves]
     copies = [
         pltpu.make_async_copy(source, target, sems.at[i])
         for i, (source, target) in enumerate(pairs)
@@ -256,12 +257,12 @@
     copies[3].wait()
     up = dot(rows_ref[...], up_ref[...])
     act = (gate / (1.0 + jnp.exp(-gate)) * up).astype(bf16)
-    copies[4].wait()
-    made = dot(act, down_ref[...]).astype(bf16)
-    o_ref[:, 0:D] = made[main]
-    o_ref[:, D:WIDE] = (
-        dot_first(low, made[rest, 0:HALF]) + dot_first(high, made[rest, HALF:D])
-    ).astype(bf16)
+    made = []
+    for copy, cols in zip(copies[4:], halves):
+        copy.wait()
+        made.append(dot(act, down_ref[:, cols]).astype(bf16))
+        o_ref[:, cols] = made[-1][main]
+    o_ref[:, D:WIDE] = (dot_first(low, made[0][rest]) + dot_first(high, made[1][rest])).astype(bf16)
 
 
 def mix_kernel(y_ref, hidden_ref, m_ref, l_ref, h_ref, o_ref):
@@ -338,7 +339,7 @@
         pltpu.VMEM((SLOT_ROWS + REST_ROWS, D), bf16),
         pltpu.VMEM((SLOT_ROWS + REST_ROWS, D), f32),
         *[pltpu.VMEM(w.shape, bf16) for w in weights],
-        pltpu.SemaphoreType.DMA((5,)),
+        pltpu.SemaphoreType.DMA((6,)),
     ]
     args = (rows, residual, norm_gain.reshape(1, D), *weights)
     outs = of(SLOT_ROWS, WIDE)

time: 212 us -> 212 us (level)
  no operation moved by 1% of the time
where the time goes in v6:
time: 212 us
  waiting for transfers between devices  122 us (58%)
  starting transfers between devices  66 us (31%)
  Pallas kernels  20 us (9%)
  local copies, waits for them, and re-layouts  2.24 us (1%)
    all_to_all x4, waiting for transfers between devices, exchange(): return lax.all_to_all(x, axes, split_axis=0, concat_axis=0, tiled=True)  76 us
    all_to_all x4, starting transfers between devices, exchange(): return lax.all_to_all(x, axes, split_axis=0, concat_axis=0, tiled=True)  42.9 us
    ppermute x3, waiting for transfers between devices, layer(): pairs[j - 1] = lax.ppermute(pairs[j - 1], ('y', 'm'), shift_pairs(j))  34 us
    pallas_call x10, Pallas kernels, call(): pl.pallas_call(kernel, out_shape=outs, in_specs=specs + [pl.BlockSpec(mem...  20 us
    ppermute x1, waiting for transfers between devices, layer(): far = lax.ppermute(far, 'y', [(i, (i + FAR) % RING) for i in range(RING)])  12 us
    ppermute x3, starting transfers between devices, layer(): pairs[j - 1] = lax.ppermute(pairs[j - 1], ('y', 'm'), shift_pairs(j))  11.6 us
  transfers between devices with their start and end apart: 11, of which 7 were waited for; matrix products, arithmetic and copies ran while one was open for 1% of the time, Pallas kernels for 4%

profile of v6, /device:TPU:1, one launch (start us, length us, event | category | flops | bytes accessed | tf_op | source)
XLA Modules:
  0.0 211.5 jit_solution(11098685888472578111)
XLA Ops:
  0.0 2.1 %shard_map.109 = bf16[24,152,128]{2,1,0:T(8,128)(2,1)} custom-call(bf16[64,1024]{1,0:T(8,128)(2,1)} %bitcast.37, bf16[64,1024]{1,0:T(8,128)(2,1)} %bitcast.38, bf16[64,1024]{1,0:T(8,128)(2,1)} %bitcast.39), custom_call_target="tpu_custom_call" | custom-call | tf_op jit(solution)/shard_map/pallas_call | solution.py:283
  2.1 18.5 %all-to-all-start = ((bf16[24,152,128]{2,1,0:T(8,128)(2,1)}), bf16[24,152,128]{2,1,0:T(8,128)(2,1)S(1)}, u32[]{:S(2)}, u32[]{:S(2)}) async-start(bf16[24,152,128]{2,1,0:T(8,128)(2,1)} %shard_map.109), calls=%async_computation | async-start | bytes 1867776 | tf_op jit(solution)/shard_map/all_to_all | solution.py:354
  20.7 0.3 shard_map.113.refs_0_
  20.9 2.2 %collective-permute-start = (bf16[64,2176]{1,0:T(8,128)(2,1)S(1)}, bf16[64,2176]{1,0:T(8,128)(2,1)S(1)}, u32[]{:S(2)}, u32[]{:S(2)}) collective-permute-start(bf16[64,2176]{1,0:T(8,128)(2,1)S(1)} %shard_map.113.refs_0_), channel_id=1, source_target_pairs={{0,2},{1,3},{2,0},{3,1},{4,6},{5,7},{6,4},{7,5},{8,10},{9,11},{10,... | collective-permute-start | bytes 835592 | tf_op jit(solution)/shard_map/ppermute | solution.py:378
  23.2 32.6 %all-to-all-done.x_ref = bf16[24,152,128]{2,1,0:T(8,128)(2,1)S(1)} async-done(((bf16[24,152,128]{2,1,0:T(8,128)(2,1)}), bf16[24,152,128]{2,1,0:T(8,128)(2,1)S(1)}, u32[]{:S(2)}, u32[]{:S(2)}) %all-to-all-start) | async-done | bytes 933920 | tf_op jit(solution)/shard_map/all_to_all | solution.py:354
  55.8 2.1 shard_map.110
  57.9 8.0 %all-to-all-start.1 = ((bf16[24,24,128]{2,1,0:T(8,128)(2,1)}), bf16[24,24,128]{2,1,0:T(8,128)(2,1)S(1)}, u32[]{:S(2)}, u32[]{:S(2)}) async-start(bf16[24,24,128]{2,1,0:T(8,128)(2,1)} %shard_map.110), calls=%async_computation.1 | async-start | bytes 294912 | tf_op jit(solution)/shard_map/all_to_all | solution.py:354
  65.8 0.9 pad_maximum_fusion.1
  66.7 3.4 %collective-permute-start.1 = (bf16[2,64,2176]{2,1,0:T(8,128)(2,1)}, bf16[2,64,2176]{2,1,0:T(8,128)(2,1)S(1)}, u32[]{:S(2)}, u32[]{:S(2)}) collective-permute-start(bf16[2,64,2176]{2,1,0:T(8,128)(2,1)} %pad_maximum_fusion.1), channel_id=1, source_target_pairs={{0,1},{1,0},{2,3},{3,2},{4,5},{5,4},{6,7},{7,6},{8,9},{9,8},{10,11... | collective-permute-start | bytes 1671176 | tf_op jit(solution)/shard_map/ppermute | solution.py:380
  70.1 0.5 shard_map.111
  70.6 7.3 %all-to-all-done.1.a_ref = bf16[24,24,128]{2,1,0:T(8,128)(2,1)S(1)} async-done(((bf16[24,24,128]{2,1,0:T(8,128)(2,1)}), bf16[24,24,128]{2,1,0:T(8,128)(2,1)S(1)}, u32[]{:S(2)}, u32[]{:S(2)}) %all-to-all-start.1) | async-done | bytes 147488 | tf_op jit(solution)/shard_map/all_to_all | solution.py:354
  77.9 1.3 shard_map.112
  79.2 10.4 %all-to-all-start.2 = ((bf16[32,8,1536]{2,1,0:T(8,128)(2,1)}), bf16[32,8,1536]{2,1,0:T(8,128)(2,1)S(1)}, u32[]{:S(2)}, u32[]{:S(2)}) async-start(bf16[32,8,1536]{2,1,0:T(8,128)(2,1)} %bitcast.8), calls=%async_computation.2 | async-start | bytes 1572864 | tf_op jit(solution)/shard_map/all_to_all | solution.py:354
  89.6 0.1 pad_add_fusion.place_ref
  89.7 1.7 shard_map.114
  91.4 3.2 %collective-permute-start.3 = (bf16[2,4,8,3072]{3,2,1,0:T(8,128)(2,1)S(1)}, bf16[2,4,8,3072]{3,2,1,0:T(8,128)(2,1)S(1)}, u32[]{:S(2)}, u32[]{:S(2)}) collective-permute-start(bf16[2,4,8,3072]{3,2,1,0:T(8,128)(2,1)S(1)} %get-tuple-element.24), channel_id=1, source_target_pairs={{0,28},{1,5},{2,30},{3,7},{4,0},{5,9},{6,2},{7,11},{8,4},{9,13},{1... | collective-permute-start | bytes 1179656 | tf_op jit(solution)/shard_map/ppermute | solution.py:384
  94.7 4.0 %collective-permute-start.4 = (bf16[2,4,8,3072]{3,2,1,0:T(8,128)(2,1)S(1)}, bf16[2,4,8,3072]{3,2,1,0:T(8,128)(2,1)S(1)}, u32[]{:S(2)}, u32[]{:S(2)}) collective-permute-start(bf16[2,4,8,3072]{3,2,1,0:T(8,128)(2,1)S(1)} %get-tuple-element.25), channel_id=1, source_target_pairs={{0,24},{1,9},{2,26},{3,11},{4,28},{5,13},{6,30},{7,15},{8,0},{9,17... | collective-permute-start | bytes 1179656 | tf_op jit(solution)/shard_map/ppermute | solution.py:384
  98.7 4.3 %collective-permute-start.5 = (bf16[2,4,8,3072]{3,2,1,0:T(8,128)(2,1)S(1)}, bf16[2,4,8,3072]{3,2,1,0:T(8,128)(2,1)S(1)}, u32[]{:S(2)}, u32[]{:S(2)}) collective-permute-start(bf16[2,4,8,3072]{3,2,1,0:T(8,128)(2,1)S(1)} %get-tuple-element.26), channel_id=1, source_target_pairs={{0,20},{1,13},{2,22},{3,15},{4,24},{5,17},{6,26},{7,19},{8,28},{9,... | collective-permute-start | bytes 1179656 | tf_op jit(solution)/shard_map/ppermute | solution.py:384
  103.1 11.4 %collective-permute-done.3.refs_0_ = bf16[2,4,8,3072]{3,2,1,0:T(8,128)(2,1)S(1)} collective-permute-done((bf16[2,4,8,3072]{3,2,1,0:T(8,128)(2,1)S(1)}, bf16[2,4,8,3072]{3,2,1,0:T(8,128)(2,1)S(1)}, u32[]{:S(2)}, u32[]{:S(2)}) %collective-permute-start.3) | collective-permute-done | bytes 393248 | tf_op jit(solution)/shard_map/ppermute | solution.py:384
  114.5 6.9 %collective-permute-done.4.refs_1_ = bf16[2,4,8,3072]{3,2,1,0:T(8,128)(2,1)S(1)} collective-permute-done((bf16[2,4,8,3072]{3,2,1,0:T(8,128)(2,1)S(1)}, bf16[2,4,8,3072]{3,2,1,0:T(8,128)(2,1)S(1)}, u32[]{:S(2)}, u32[]{:S(2)}) %collective-permute-start.4) | collective-permute-done | bytes 393248 | tf_op jit(solution)/shard_map/ppermute | solution.py:384
  121.4 15.7 %collective-permute-done.5.refs_2_ = bf16[2,4,8,3072]{3,2,1,0:T(8,128)(2,1)S(1)} collective-permute-done((bf16[2,4,8,3072]{3,2,1,0:T(8,128)(2,1)S(1)}, bf16[2,4,8,3072]{3,2,1,0:T(8,128)(2,1)S(1)}, u32[]{:S(2)}, u32[]{:S(2)}) %collective-permute-start.5) | collective-permute-done | bytes 393248 | tf_op jit(solution)/shard_map/ppermute | solution.py:384
  137.1 0.1 pad_maximum_fusion
  137.2 1.9 collective-permute-start.6
  139.1 4.0 %collective-permute-start.2 = (bf16[4,8,3072]{2,1,0:T(8,128)(2,1)S(1)}, bf16[4,8,3072]{2,1,0:T(8,128)(2,1)S(1)}, u32[]{:S(2)}, u32[]{:S(2)}) collective-permute-start(bf16[4,8,3072]{2,1,0:T(8,128)(2,1)S(1)} %get-tuple-element.23), channel_id=1, source_target_pairs={{0,16},{4,20},{8,24},{12,28},{16,0},{20,4},{24,8},{28,12},{1,17},{... | collective-permute-start | bytes 589832 | tf_op jit(solution)/shard_map/ppermute | solution.py:382
  143.1 12.0 %collective-permute-done.2.far_ref = bf16[4,8,3072]{2,1,0:T(8,128)(2,1)S(1)} collective-permute-done((bf16[4,8,3072]{2,1,0:T(8,128)(2,1)S(1)}, bf16[4,8,3072]{2,1,0:T(8,128)(2,1)S(1)}, u32[]{:S(2)}, u32[]{:S(2)}) %collective-permute-start.2) | collective-permute-done | bytes 196640 | tf_op jit(solution)/shard_map/ppermute | solution.py:382
  155.1 1.0 shard_map.115.residual_ref
  156.1 8.8 %shard_map.116 = bf16[256,3072]{1,0:T(8,128)(2,1)} custom-call(bf16[256,1536]{1,0:T(8,128)(2,1)S(1)} %bitcast.25, bf16[384,2048]{1,0:T(8,128)(2,1)S(1)} %shard_map.115.residual_ref, f32[1,2048]{1,0:T(1,128)S(1)} %bitcast.30, bf16[1024,2048]{1,0:T(8,128)(2,1)} %w_ref.1, bf16[2048,512]{1,0:T(8,128)(2,1)} %bitcast.34, bf16[2048,512]{1,0:T(8,128)(2,1)} %bitcast.35, ...), custom_call_target="tpu_custom_call" | custom-call | tf_op jit(solution)/shard_map/pallas_call | solution.py:283
  164.9 6.1 %all-to-all-start.3 = ((bf16[32,8,3072]{2,1,0:T(8,128)(2,1)}), bf16[32,8,3072]{2,1,0:T(8,128)(2,1)S(1)}, u32[]{:S(2)}, u32[]{:S(2)}) async-start(bf16[32,8,3072]{2,1,0:T(8,128)(2,1)} %bitcast.20), calls=%async_computation.3 | async-start | bytes 3145728 | tf_op jit(solution)/shard_map/all_to_all | solution.py:354
  171.1 2.2 %copy-done = bf16[1024,2048]{1,0:T(8,128)(2,1)S(1)} copy-done((bf16[1024,2048]{1,0:T(8,128)(2,1)S(1)}, bf16[1024,2048]{1,0:T(8,128)(2,1)}, u32[]{:S(2)}) %copy-start) | copy-done | bytes 4194328
  173.2 0.8 shard_map.117.hidden_ref
  174.1 36.1 %all-to-all-done.3 = bf16[32,8,3072]{2,1,0:T(8,128)(2,1)S(1)} async-done(((bf16[32,8,3072]{2,1,0:T(8,128)(2,1)}), bf16[32,8,3072]{2,1,0:T(8,128)(2,1)S(1)}, u32[]{:S(2)}, u32[]{:S(2)}) %all-to-all-start.3) | async-done | bytes 1572896 | tf_op jit(solution)/shard_map/all_to_all | solution.py:354
  210.2 1.3 shard_map.118
  (16 shorter events, 0.1 us)
Async XLA Ops:
  0.0 20.7 %copy-start.3 = (s32[1,64,4]{1,2,0:T(4,128)S(1)}, s32[1,64,4]{1,2,0:T(4,128)}, u32[]{:S(2)}) copy-start(s32[1,64,4]{1,2,0:T(4,128)} %param.20) | copy-start | bytes 3076
  0.0 20.7 %copy-start.1 = (bf16[1,64,2048]{2,1,0:T(8,128)(2,1)S(1)}, bf16[1,64,2048]{2,1,0:T(8,128)(2,1)}, u32[]{:S(2)}) copy-start(bf16[1,64,2048]{2,1,0:T(8,128)(2,1)} %param.14) | copy-start | bytes 786436
  2.1 67.9 %copy-start.4 = (f32[1,64,4]{1,2,0:T(4,128)S(1)}, f32[1,64,4]{1,2,0:T(4,128)}, u32[]{:S(2)}) copy-start(f32[1,64,4]{1,2,0:T(4,128)} %param.21) | copy-start | bytes 3076
  2.1 53.6 %all-to-all-start = ((bf16[24,152,128]{2,1,0:T(8,128)(2,1)}), bf16[24,152,128]{2,1,0:T(8,128)(2,1)S(1)}, u32[]{:S(2)}, u32[]{:S(2)}) async-start(bf16[24,152,128]{2,1,0:T(8,128)(2,1)} %shard_map.109), calls=%async_computation | async-start | bytes 1867776 | tf_op jit(solution)/shard_map/all_to_all | solution.py:354
  20.9 44.9 %collective-permute-start = (bf16[64,2176]{1,0:T(8,128)(2,1)S(1)}, bf16[64,2176]{1,0:T(8,128)(2,1)S(1)}, u32[]{:S(2)}, u32[]{:S(2)}) collective-permute-start(bf16[64,2176]{1,0:T(8,128)(2,1)S(1)} %shard_map.113.refs_0_), channel_id=1, source_target_pairs={{0,2},{1,3},{2,0},{3,1},{4,6},{5,7},{6,4},{7,5},{8,10},{9,11},{10,... | collective-permute-start | bytes 835592 | tf_op jit(solution)/shard_map/ppermute | solution.py:378
  57.9 20.0 %all-to-all-start.1 = ((bf16[24,24,128]{2,1,0:T(8,128)(2,1)}), bf16[24,24,128]{2,1,0:T(8,128)(2,1)S(1)}, u32[]{:S(2)}, u32[]{:S(2)}) async-start(bf16[24,24,128]{2,1,0:T(8,128)(2,1)} %shard_map.110), calls=%async_computation.1 | async-start | bytes 294912 | tf_op jit(solution)/shard_map/all_to_all | solution.py:354
  66.7 23.0 %collective-permute-start.1 = (bf16[2,64,2176]{2,1,0:T(8,128)(2,1)}, bf16[2,64,2176]{2,1,0:T(8,128)(2,1)S(1)}, u32[]{:S(2)}, u32[]{:S(2)}) collective-permute-start(bf16[2,64,2176]{2,1,0:T(8,128)(2,1)} %pad_maximum_fusion.1), channel_id=1, source_target_pairs={{0,1},{1,0},{2,3},{3,2},{4,5},{5,4},{6,7},{7,6},{8,9},{9,8},{10,11... | collective-permute-start | bytes 1671176 | tf_op jit(solution)/shard_map/ppermute | solution.py:380
  79.2 76.9 %all-to-all-start.2 = ((bf16[32,8,1536]{2,1,0:T(8,128)(2,1)}), bf16[32,8,1536]{2,1,0:T(8,128)(2,1)S(1)}, u32[]{:S(2)}, u32[]{:S(2)}) async-start(bf16[32,8,1536]{2,1,0:T(8,128)(2,1)} %bitcast.8), calls=%async_computation.2 | async-start | bytes 1572864 | tf_op jit(solution)/shard_map/all_to_all | solution.py:354
  91.4 23.1 %collective-permute-start.3 = (bf16[2,4,8,3072]{3,2,1,0:T(8,128)(2,1)S(1)}, bf16[2,4,8,3072]{3,2,1,0:T(8,128)(2,1)S(1)}, u32[]{:S(2)}, u32[]{:S(2)}) collective-permute-start(bf16[2,4,8,3072]{3,2,1,0:T(8,128)(2,1)S(1)} %get-tuple-element.24), channel_id=1, source_target_pairs={{0,28},{1,5},{2,30},{3,7},{4,0},{5,9},{6,2},{7,11},{8,4},{9,13},{1... | collective-permute-start | bytes 1179656 | tf_op jit(solution)/shard_map/ppermute | solution.py:384
  94.7 26.7 %collective-permute-start.4 = (bf16[2,4,8,3072]{3,2,1,0:T(8,128)(2,1)S(1)}, bf16[2,4,8,3072]{3,2,1,0:T(8,128)(2,1)S(1)}, u32[]{:S(2)}, u32[]{:S(2)}) collective-permute-start(bf16[2,4,8,3072]{3,2,1,0:T(8,128)(2,1)S(1)} %get-tuple-element.25), channel_id=1, source_target_pairs={{0,24},{1,9},{2,26},{3,11},{4,28},{5,13},{6,30},{7,15},{8,0},{9,17... | collective-permute-start | bytes 1179656 | tf_op jit(solution)/shard_map/ppermute | solution.py:384
  98.7 38.3 %collective-permute-start.5 = (bf16[2,4,8,3072]{3,2,1,0:T(8,128)(2,1)S(1)}, bf16[2,4,8,3072]{3,2,1,0:T(8,128)(2,1)S(1)}, u32[]{:S(2)}, u32[]{:S(2)}) collective-permute-start(bf16[2,4,8,3072]{3,2,1,0:T(8,128)(2,1)S(1)} %get-tuple-element.26), channel_id=1, source_target_pairs={{0,20},{1,13},{2,22},{3,15},{4,24},{5,17},{6,26},{7,19},{8,28},{9,... | collective-permute-start | bytes 1179656 | tf_op jit(solution)/shard_map/ppermute | solution.py:384
  137.2 19.0 %copy-start.2 = (f32[2048]{0:T(1024)S(1)}, f32[2048]{0:T(1024)}, u32[]{:S(2)}) copy-start(f32[2048]{0:T(1024)} %param.16) | copy-start | bytes 24580
  137.2 17.9 %collective-permute-start.6 = (bf16[3,4,8,3072]{3,2,1,0:T(8,128)(2,1)S(1)}, bf16[3,4,8,3072]{3,2,1,0:T(8,128)(2,1)S(1)}, u32[]{:S(2)}, u32[]{:S(2)}) collective-permute-start(bf16[3,4,8,3072]{3,2,1,0:T(8,128)(2,1)S(1)} %pad_maximum_fusion), channel_id=1, source_target_pairs={{0,1},{1,0},{2,3},{3,2},{4,5},{5,4},{6,7},{7,6},{8,9},{9,8},{10,11... | collective-permute-start | bytes 1769480 | tf_op jit(solution)/shard_map/ppermute | solution.py:392
  139.1 16.0 %collective-permute-start.2 = (bf16[4,8,3072]{2,1,0:T(8,128)(2,1)S(1)}, bf16[4,8,3072]{2,1,0:T(8,128)(2,1)S(1)}, u32[]{:S(2)}, u32[]{:S(2)}) collective-permute-start(bf16[4,8,3072]{2,1,0:T(8,128)(2,1)S(1)} %get-tuple-element.23), channel_id=1, source_target_pairs={{0,16},{4,20},{8,24},{12,28},{16,0},{20,4},{24,8},{28,12},{1,17},{... | collective-permute-start | bytes 589832 | tf_op jit(solution)/shard_map/ppermute | solution.py:382
  164.9 45.3 %all-to-all-start.3 = ((bf16[32,8,3072]{2,1,0:T(8,128)(2,1)}), bf16[32,8,3072]{2,1,0:T(8,128)(2,1)S(1)}, u32[]{:S(2)}, u32[]{:S(2)}) async-start(bf16[32,8,3072]{2,1,0:T(8,128)(2,1)} %bitcast.20), calls=%async_computation.3 | async-start | bytes 3145728 | tf_op jit(solution)/shard_map/all_to_all | solution.py:354
  171.0 2.2 %copy-start = (bf16[1024,2048]{1,0:T(8,128)(2,1)S(1)}, bf16[1024,2048]{1,0:T(8,128)(2,1)}, u32[]{:S(2)}) copy-start(bf16[1024,2048]{1,0:T(8,128)(2,1)} %w_ref.1) | copy-start | bytes 12582916
